TPU v7x, 128 devices: a whole 4x4x4 slice. The times are simulated.
128 devices in a mesh: ccd: 8 (over y, core), strip: 16 (over z, x).
Axes of the slice: x: 4, y: 4, z: 4, core: 2. Of those that a mesh axis runs over, the one named last changes fastest.
Arguments:
- tile_store: float32 [2304, 16, 128], P(('ccd', 'strip')), may hold values from -13 to 13
- tile_source: int32 [128, 18], replicated, may hold values from 0 to 127, as said below
- tile_slot: int32 [128, 18], replicated, may hold values from 0 to 17, as said below
- shift_cols: int32 [8], P('ccd'), may hold values from -117 to 117
- spatial_order: int32 [8], P('ccd'), may hold values from 0 to 2
- science: float32 [2048, 2048], P(('ccd', 'strip')), may hold values from -16 to 16
Outputs:
- difference: float32 [2048, 2048], P(('ccd', 'strip'))
Inputs may be any that keep to these rules, and one draw needn't show every extreme that they name: `tile_source`: every device holds exactly 18 tiles over all strips, one device holds at most 1 tiles of one strip, and some device holds exactly 1 tiles of some strip. `tile_slot`: each position of each store is named by exactly one pair of strip and tile.
All inputs are finite; a program needn't handle non-finite values.
Results may differ from a plain program's by a relative error of at most 0.005.
Values sent between devices are 32-bit elements; how exact they have to be, the bound alone decides.
A program may use at most 64 MiB of HBM per device.

v0:
```python
import jax
import jax.numpy as jnp
import numpy as np
from jax import lax
from jax.experimental import pallas as pl
from jax.experimental.pallas import tpu as pltpu
from jax.sharding import PartitionSpec as P

H = 11
CM = 128
ROWS = 16
COLS = 2048
TC = 128
SLOTS = 40
TARGET = 28
ONES = 15

sigmas = (0.7, 1.5, 3.0)
tops = (4, 2, 2)
mono = ((0, 0), (1, 0), (0, 1), (2, 0), (1, 1), (0, 2))
ridge = 0.05
F32 = jnp.float32
BF16 = jnp.bfloat16


def tap_table():
    a = np.arange(-H, H + 1).astype(np.float64)
    rows = []
    for s, top in zip(sigmas, tops):
        e = np.exp(-a * a / (2.0 * s * s))
        for n in range(top + 1):
            rows.append(e * (a / s) ** n / e.sum())
    return np.stack(rows).astype(np.float32)


def to_bf16(x):
    return x.astype(jnp.bfloat16.dtype)


def band_matrix():
    taps = tap_table()
    hi = to_bf16(taps).astype(np.float32)
    lo = to_bf16(taps - hi).astype(np.float32)
    full = []
    for part in (hi, lo):
        m = np.zeros((160, 11, TC), np.float32)
        for f in range(11):
            for x in range(TC):
                m[x : x + 23, f, x] = part[f]
        full.append(m.reshape(160, 11 * TC))
    h, l = full
    tail = np.zeros((TC, 11 * TC), np.float32)
    tail[0:32], tail[32:64], tail[64:96] = h[128:], h[128:], l[128:]
    return to_bf16(np.concatenate([h[:128], h[:128], l[:128], tail]))


def slot_of(row):
    return 16 + row if row < H else (row - H if row < H + ROWS else row)


def vertical_matrices():
    taps = to_bf16(tap_table()).astype(np.float32)
    first = np.zeros((ROWS, 16, 208), np.float32)
    second = np.zeros((ROWS, 16, 240), np.float32)
    slot = 0
    for i in range(5):
        for j in range(5 - i):
            for r in range(ROWS):
                for a in range(23):
                    first[r, slot, i * SLOTS + slot_of(r + a)] = taps[j, a]
            slot += 1
    first[:, ONES, 38] = 1.0
    slot = 0
    for g in range(2):
        for i in range(3):
            for j in range(3 - i):
                for r in range(ROWS):
                    for a in range(23):
                        second[r, slot, (3 * g + i) * SLOTS + slot_of(r + a)] = taps[5 + 3 * g + j, a]
                slot += 1
    return to_bf16(first.reshape(256, 208)), to_bf16(second.reshape(256, 240))


def column_powers():
    u = 2.0 * (np.arange(COLS).astype(np.float32) + np.float32(0.5)) / np.float32(COLS) - np.float32(1.0)
    u = u.astype(np.float32)
    return np.stack([u, u * u] + [np.zeros_like(u)] * 6)


def fit_kernel(scal, own, above, below, sci, band, va, vb, upow, e_out, mom_out, rolled, hs, acc):
    shift = scal[0]
    first_row = scal[1]
    start = CM + shift - H
    tile = lax.shift_right_logical(start, 7)
    rem = lax.bitwise_and(start, 127)
    count = own.shape[0]
    row16 = lax.broadcasted_iota(jnp.int32, (1, 16, TC), 1)
    row8 = lax.broadcasted_iota(jnp.int32, (1, 8, TC), 1)
    a = pltpu.roll(above[...], H, 1)
    b = pltpu.roll(below[...], H, 1)
    mid = jnp.where(row16 < H, a, b)
    end = jnp.where(row8 < 6, b[:, :8], jnp.where(row8 == 6, 1.0, 0.0))
    x = jnp.concatenate([own[...], mid, end], axis=1)
    rolled[0:count] = pltpu.roll(x, lax.bitwise_and(128 - rem, 127), 2)
    rolled[count : count + 1] = jnp.zeros((1, SLOTS, TC), F32)
    lane3 = lax.broadcasted_iota(jnp.int32, (1, SLOTS, TC), 2)
    w = jnp.where(
        lane3 < 128 - rem, rolled[pl.ds(tile, 17)], rolled[pl.ds(tile + 1, 17)]
    ).reshape(17 * SLOTS, TC)
    main = w[: 16 * SLOTS]
    nxt = w[SLOTS:]
    hi = main.astype(BF16)
    lo = (main - hi.astype(F32)).astype(BF16)
    nhi = nxt.astype(BF16).astype(F32)
    nlo = nxt - nhi
    lane = lax.broadcasted_iota(jnp.int32, (1, TC), 1)
    tail = jnp.where(
        lane < 32,
        nhi,
        jnp.where(lane < 64, pltpu.roll(nlo, 32, 1), jnp.where(lane < 96, pltpu.roll(nhi, 64, 1), 0.0)),
    ).astype(BF16)
    lhs = jnp.concatenate([hi, lo, hi, tail], axis=1)
    for c in range(6):
        n = 256 if c < 5 else 128
        res = jnp.dot(lhs, band[:, 256 * c : 256 * c + n], preferred_element_type=F32)
        for f in range(2 * c, 2 * c + n // TC):
            o = (f - 2 * c) * TC
            for j in range(16):
                hs[f * SLOTS : (f + 1) * SLOTS, j * TC : (j + 1) * TC] = res[
                    j * SLOTS : (j + 1) * SLOTS, o : o + TC
                ]
    for c in range(8):
        cols = slice(256 * c, 256 * c + 256)
        oa = jnp.dot(va[...], hs[0:208, cols].astype(BF16), preferred_element_type=F32)
        ob = jnp.dot(vb[...], hs[200:440, cols].astype(BF16), preferred_element_type=F32)
        e = jnp.concatenate([oa.reshape(ROWS, 16, 256), ob.reshape(ROWS, 16, 256)], axis=1)
        e_out[:, cols] = e.reshape(ROWS * 32, 256).astype(BF16)
    acc[...] = jnp.zeros_like(acc)
    u1 = upow[0:1, :]
    u2 = upow[1:2, :]
    brow = lax.broadcasted_iota(jnp.int32, (32, 1), 0)

    def row_step(r, carry):
        e = e_out[pl.ds(pl.multiple_of(r * 32, 32), 32), :].astype(F32)
        e = jnp.where(brow == TARGET, sci[pl.ds(r, 1), :], e)
        e16 = e.astype(BF16)
        e = e16.astype(F32)
        f1 = (e * u1).astype(BF16)
        f2 = (e * u2).astype(BF16)
        g = lax.dot_general(
            jnp.concatenate([e16, f2], axis=0),
            jnp.concatenate([e16, f1, f2], axis=0),
            (((1,), (1,)), ((), ())),
            preferred_element_type=F32,
        )
        v = (first_row + r).astype(F32) * (2.0 / 256.0) + (1.0 / 256.0 - 1.0)
        scale = 1.0
        for m in range(5):
            n = 64 if m < 2 else 32
            acc[m, 0:n, 0:96] += g[0:n] * scale
            scale = scale * v
        return carry

    lax.fori_loop(0, ROWS, row_step, 0)
    units = (
        jnp.where(lane < 96, acc[0, 0:32], pltpu.roll(acc[0, 32:64], 64, 1)),
        jnp.where(lane < 96, acc[1, 0:32], pltpu.roll(acc[1, 32:64], 64, 1)),
        jnp.where(lane < 96, acc[2, 0:32], pltpu.roll(acc[0, 32:64], 32, 1)),
        jnp.where(lane < 64, acc[3, 0:32], pltpu.roll(acc[4, 0:32], 64, 1)),
    )
    for i, unit in enumerate(units):
        mom_out[32 * i : 32 * i + 32] = unit


def unit_of(k, m):
    if m < 2 and k < 4:
        return m, k
    if m == 2:
        return 2, k
    return {(4, 0): (2, 3), (0, 3): (3, 0), (1, 3): (3, 1), (0, 4): (3, 2)}[(k, m)]


def apply_kernel(scal, moms, e_ref, sci, upow, out, mat, fx):
    order = scal[2]
    first_row = scal[1]
    total = moms[0]
    for i in range(1, moms.shape[0]):
        total = total + moms[i]
    units = [total[32 * i : 32 * i + 32] for i in range(4)]
    lane = lax.broadcasted_iota(jnp.int32, (1, TC), 1)
    row = lax.broadcasted_iota(jnp.int32, (32, 1), 0)
    degree = lambda q: 0 if q == 0 else (1 if q < 3 else 2)

    def col_active(t):
        q = lax.shift_right_logical(lane, 5) + 4 * t
        deg = jnp.where(q >= 1, 1, 0) + jnp.where(q >= 3, 1, 0)
        return (deg <= order) | (lax.bitwise_and(lane, 31) == ONES)

    for q in range(6):
        row_on = (degree(q) <= order) | (row == ONES)
        for t in range(2):
            block = jnp.zeros((32, TC), F32)
            for s in range(4 if t == 0 else 2):
                p = 4 * t + s
                i, k = unit_of(mono[q][0] + mono[p][0], mono[q][1] + mono[p][1])
                piece = units[i]
                if s != k:
                    piece = pltpu.roll(piece, (32 * (s - k)) % 128, 1)
                block = jnp.where(lax.shift_right_logical(lane, 5) == s, piece, block)
            both = row_on & col_active(t)
            block = jnp.where(both, block, 0.0)
            if t == q // 4:
                diag = lane == row + 32 * (q % 4)
                block = jnp.where(diag, jnp.where(both, block, 1.0) * (1.0 + ridge), block)
            mat[32 * q : 32 * q + 32, TC * t : TC * t + TC] = block
            if q == 0:
                mat[192:200, TC * t : TC * t + TC] = jnp.where(col_active(t), block[24:32], 0.0)
    wide = lax.broadcasted_iota(jnp.int32, (1, 2 * TC), 1)
    for q in range(6):
        t = q // 4
        top = 32 * q
        base = 32 * (q % 4)

        def sweep(b, carry, t=t, top=top, base=base):
            panel = mat[top : top + 32, :]
            prow = mat[pl.ds(top + b, 1), :]
            at = lane == base + b
            col = jnp.sum(
                jnp.where(at, panel[:, TC * t : TC * t + TC], 0.0), axis=1, keepdims=True
            )
            d = jnp.sum(jnp.where(at, prow[:, TC * t : TC * t + TC], 0.0), axis=1, keepdims=True)
            inv = 1.0 / d
            here = row == b
            g = jnp.where(here, -1.0, col) * inv
            atw = wide == TC * t + base + b
            mat[top : top + 32, :] = jnp.where(atw | here, 0.0, panel) - g * jnp.where(atw, 1.0, prow)
            return carry

        lax.fori_loop(0, 28, sweep, 0)
        panel = mat[top : top + 32, :]
        local = wide - (TC * t + base)
        inside = (local >= 0) & (local < 28)
        f = jnp.where(row < 28, jnp.where(inside, -panel, panel), 0.0)
        fx[...] = jnp.zeros_like(fx)
        fx[base : base + 32, :] = f
        rest = mat[top + 32 : 200, :]
        mat[top + 32 : 200, :] = jnp.where(inside, 0.0, rest) - jnp.dot(
            rest[:, TC * t : TC * t + TC],
            fx[...],
            preferred_element_type=F32,
            precision=lax.Precision.HIGHEST,
        )
    coef = []
    for q in range(6):
        z = mat[192:200, TC * (q // 4) : TC * (q // 4) + TC]
        z = jnp.broadcast_to(z[TARGET - 24 : TARGET - 23], (8, TC))
        if q % 4:
            z = pltpu.roll(z, 128 - 32 * (q % 4), 1)
        z = jnp.where(lane < 28, z, 0.0)
        z = z + pltpu.roll(z, 32, 1)
        z = z + pltpu.roll(z, 64, 1)
        coef.append(jnp.concatenate([z, z], axis=0))
    row16 = lax.broadcasted_iota(jnp.int32, (16, 1), 0)
    v = (first_row + row16).astype(F32) * (2.0 / 256.0) + (1.0 / 256.0 - 1.0)
    parts = (coef[0] + v * (coef[2] + v * coef[5]), coef[1] + v * coef[4], coef[3])
    his, los = [], []
    for p in parts:
        wide_p = jnp.concatenate(
            [jnp.where(row16 == 4 * n + lax.shift_right_logical(lane, 5), p, 0.0) for n in range(4)],
            axis=1,
        )
        h = wide_p.astype(BF16)
        his.append(h)
        los.append((wide_p - h.astype(F32)).astype(BF16))
    res = jnp.dot(jnp.concatenate(his + los, axis=0), e_ref[...], preferred_element_type=F32)
    t0, t1, t2 = (res[16 * i : 16 * i + 16] + res[48 + 16 * i : 64 + 16 * i] for i in range(3))
    u = upow[0:1, :]
    out[...] = sci[...] - (t0 + u * (t1 + u * t2))


VM = pl.BlockSpec(memory_space=pltpu.VMEM)
SM = pl.BlockSpec(memory_space=pltpu.SMEM)
LIMIT = 60 * 1024 * 1024


def fit(scal, own, above, below, sci):
    band = jnp.asarray(band_matrix())
    va, vb = (jnp.asarray(m) for m in vertical_matrices())
    upow = jnp.asarray(column_powers())
    return pl.pallas_call(
        fit_kernel,
        out_shape=(
            jax.ShapeDtypeStruct((ROWS * 32, COLS), BF16),
            jax.ShapeDtypeStruct((128, TC), F32),
        ),
        in_specs=[SM] + [VM] * 8,
        out_specs=(VM, VM),
        scratch_shapes=[
            pltpu.VMEM((own.shape[0] + 1, SLOTS, TC), F32),
            pltpu.VMEM((440, COLS), F32),
            pltpu.VMEM((5, 64, TC), F32),
        ],
        compiler_params=pltpu.CompilerParams(vmem_limit_bytes=LIMIT),
        name="fit",
    )(scal, own, above, below, sci, band, va, vb, upow)


def apply(scal, moms, e, sci):
    upow = jnp.asarray(column_powers())
    return pl.pallas_call(
        apply_kernel,
        out_shape=jax.ShapeDtypeStruct((ROWS, COLS), F32),
        in_specs=[SM] + [VM] * 4,
        out_specs=VM,
        scratch_shapes=[pltpu.VMEM((200, 2 * TC), F32), pltpu.VMEM((TC, 2 * TC), F32)],
        compiler_params=pltpu.CompilerParams(vmem_limit_bytes=LIMIT),
        name="apply",
    )(scal, moms, e, sci, upow)


def body(tile_store, tile_source, tile_slot, shift_cols, spatial_order, science):
    strips = lax.axis_size("strip")
    strip = lax.axis_index("strip")
    me = lax.axis_index("ccd") * strips + strip
    pick = jnp.sum(jnp.where(tile_source == me, tile_slot, 0), axis=1)
    outgoing = jnp.take(tile_store, pick, axis=0)
    arrived = lax.all_to_all(outgoing, ("ccd", "strip"), split_axis=0, concat_axis=0, tiled=True)
    owner = lax.dynamic_index_in_dim(tile_source, me, 0, keepdims=False)
    own = jnp.take(arrived, owner, axis=0)
    above = lax.ppermute(own, "strip", [(i, i + 1) for i in range(strips - 1)])
    below = lax.ppermute(own, "strip", [(i + 1, i) for i in range(strips - 1)])
    scal = jnp.stack([shift_cols[0], strip * ROWS, spatial_order[0]]).astype(jnp.int32)
    e, mom = fit(scal, own, above, below, science)
    moms = lax.all_to_all(
        jnp.broadcast_to(mom[None], (strips, *mom.shape)), "strip", 0, 0, tiled=True
    )
    return apply(scal, moms, e, science)


def solution(mesh):
    placed = (
        P(("ccd", "strip"), None, None),
        P(),
        P(),
        P("ccd"),
        P("ccd"),
        P(("ccd", "strip"), None),
    )
    return jax.shard_map(
        body, mesh=mesh, in_specs=placed, out_specs=P(("ccd", "strip"), None), check_vma=False
    )
```

profile of v0, /device:TPU:0, one launch (start us, length us, event | category | flops | bytes accessed | tf_op | source)
XLA Modules:
  0.0 98.1 jit_solution(6605120473551707540)
XLA Ops:
  0.0 0.0 copy-start
  0.0 0.8 select_reduce_fusion
  0.8 0.1 copy-done
  0.9 0.8 gather_fusion
  1.7 0.0 copy-start.4
  1.7 1.2 %broadcast_select_fusion = f32[128,16,128]{2,1,0:T(8,128)} fusion(f32[128,16,128]{2,1,0:T(8,128)S(1)} %gather_fusion, pred[128]{0:T(512)(128)(4,1)S(1)} %compare_and_fusion), kind=kLoop, calls=%fused_computation.2 | loop fusion | flops 262144 | bytes 2097280 | tf_op jit(solution)/shard_map/jit(_take)/select_n | solution.py:326
  2.9 11.2 %all-to-all-start = ((f32[128,16,128]{2,1,0:T(8,128)}), f32[128,16,128]{2,1,0:T(8,128)S(1)}, u32[]{:S(2)}, u32[]{:S(2)}) async-start(f32[128,16,128]{2,1,0:T(8,128)} %broadcast_select_fusion), calls=%async_computation | async-start | bytes 2097152 | tf_op jit(solution)/shard_map/all_to_all | solution.py:327
  14.1 0.0 copy-done.4
  14.1 0.2 dynamic-slice_reduce_fusion
  14.3 18.8 %all-to-all-done = f32[128,16,128]{2,1,0:T(8,128)S(1)} async-done(((f32[128,16,128]{2,1,0:T(8,128)}), f32[128,16,128]{2,1,0:T(8,128)S(1)}, u32[]{:S(2)}, u32[]{:S(2)}) %all-to-all-start) | async-done | bytes 1048608 | tf_op jit(solution)/shard_map/all_to_all | solution.py:327
  33.1 0.6 gather_fusion.1
  33.7 0.1 broadcast_select_fusion.1.own
  33.8 0.0 copy-start.1
  33.8 1.3 %collective-permute-start.1 = (f32[18,16,128]{2,1,0:T(8,128)S(1)}, f32[18,16,128]{2,1,0:T(8,128)S(1)}, u32[]{:S(2)}, u32[]{:S(2)}) collective-permute-start(f32[18,16,128]{2,1,0:T(8,128)S(1)} %broadcast_select_fusion.1.own), channel_id=1, source_target_pairs={{1,0},{2,1},{3,2},{4,3},{5,4},{6,5},{7,6},{8,7},{9,8},{10,9},{11,1... | collective-permute-start | bytes 442376 | tf_op jit(solution)/shard_map/ppermute | solution.py:331
  35.1 4.6 %collective-permute-start = (f32[18,16,128]{2,1,0:T(8,128)S(1)}, f32[18,16,128]{2,1,0:T(8,128)S(1)}, u32[]{:S(2)}, u32[]{:S(2)}) collective-permute-start(f32[18,16,128]{2,1,0:T(8,128)S(1)} %broadcast_select_fusion.1.own), channel_id=1, source_target_pairs={{0,1},{1,2},{2,3},{3,4},{4,5},{5,6},{6,7},{7,8},{8,9},{9,10},{10,1... | collective-permute-start | bytes 442376 | tf_op jit(solution)/shard_map/ppermute | solution.py:330
  40.9 0.6 pad_add_fusion.scal
  41.6 0.0 collective-permute-done.1.below
  41.6 0.8 collective-permute-done.above
  42.4 0.0 copy-done.2
  42.4 0.6 copy-done.3
  43.0 9.0 %fit.1 = (bf16[512,2048]{1,0:T(8,128)(2,1)}, f32[128,128]{1,0:T(8,128)}) custom-call(s32[3]{0:T(128)} %pad_add_fusion.scal, f32[18,16,128]{2,1,0:T(8,128)} %copy-done.1, f32[18,16,128]{2,1,0:T(8,128)} %copy-done.3, f32[18,16,128]{2,1,0:T(8,128)} %copy-done.2, f32[16,2048]{1,0:T(8,128)} %sci.3, bf16[512,1408]{1,0:T(8,128)(2,1)} %constant.54.clone.band, ...), custom_call_target="tpu_custom_call" | custom-call | tf_op jit(solution)/shard_map/fit/pallas_call | solution.py:290
  52.0 0.9 broadcast_in_dim.35
  53.0 24.0 %all_to_all.10.moms = f32[16,128,128]{2,1,0:T(8,128)} all-to-all(f32[16,128,128]{2,1,0:T(8,128)S(1)} %broadcast_in_dim.35), channel_id=1, replica_groups=mesh['ccd'=8,'strip'=16] {'strip'}, dimensions={0} | all-to-all | bytes 2097152 | tf_op jit(solution)/shard_map/all_to_all | solution.py:334
  76.9 21.1 %apply.1 = f32[16,2048]{1,0:T(8,128)} custom-call(s32[3]{0:T(128)} %pad_add_fusion.scal, f32[16,128,128]{2,1,0:T(8,128)} %all_to_all.10.moms, bf16[512,2048]{1,0:T(8,128)(2,1)} %get-tuple-element.8.e_ref, f32[16,2048]{1,0:T(8,128)} %sci.3, f32[8,2048]{1,0:T(8,128)} %constant.57.clone.upow), custom_call_target="tpu_custom_call" | custom-call | tf_op jit(solution)/shard_map/apply/pallas_call | solution.py:310
  (9 shorter events, 0.0 us)
Async XLA Ops:
  0.0 0.9 copy-start
  1.7 12.4 %copy-start.4 = (s32[128,18]{0,1:T(8,128)S(1)}, s32[128,18]{0,1:T(8,128)}, u32[]{:S(2)}) copy-start(s32[128,18]{0,1:T(8,128)} %param.12) | copy-start | bytes 27652
  2.9 30.2 %all-to-all-start = ((f32[128,16,128]{2,1,0:T(8,128)}), f32[128,16,128]{2,1,0:T(8,128)S(1)}, u32[]{:S(2)}, u32[]{:S(2)}) async-start(f32[128,16,128]{2,1,0:T(8,128)} %broadcast_select_fusion), calls=%async_computation | async-start | bytes 2097152 | tf_op jit(solution)/shard_map/all_to_all | solution.py:327
  33.8 8.6 %copy-start.1 = (f32[18,16,128]{2,1,0:T(8,128)}, f32[18,16,128]{2,1,0:T(8,128)S(1)}, u32[]{:S(2)}) copy-start(f32[18,16,128]{2,1,0:T(8,128)S(1)} %broadcast_select_fusion.1.own) | copy-start | bytes 442372
  33.8 7.8 %collective-permute-start.1 = (f32[18,16,128]{2,1,0:T(8,128)S(1)}, f32[18,16,128]{2,1,0:T(8,128)S(1)}, u32[]{:S(2)}, u32[]{:S(2)}) collective-permute-start(f32[18,16,128]{2,1,0:T(8,128)S(1)} %broadcast_select_fusion.1.own), channel_id=1, source_target_pairs={{1,0},{2,1},{3,2},{4,3},{5,4},{6,5},{7,6},{8,7},{9,8},{10,9},{11,1... | collective-permute-start | bytes 442376 | tf_op jit(solution)/shard_map/ppermute | solution.py:331
  35.1 7.3 %collective-permute-start = (f32[18,16,128]{2,1,0:T(8,128)S(1)}, f32[18,16,128]{2,1,0:T(8,128)S(1)}, u32[]{:S(2)}, u32[]{:S(2)}) collective-permute-start(f32[18,16,128]{2,1,0:T(8,128)S(1)} %broadcast_select_fusion.1.own), channel_id=1, source_target_pairs={{0,1},{1,2},{2,3},{3,4},{4,5},{5,6},{6,7},{7,8},{8,9},{9,10},{10,1... | collective-permute-start | bytes 442376 | tf_op jit(solution)/shard_map/ppermute | solution.py:330
  41.6 0.8 copy-start.2
  42.4 0.6 copy-start.3
where the time goes:
time: 98.5 us; the launch traced here: 98.1 us
  Pallas kernels  30.1 us (31%)
  blocking collectives  24 us (24%)
  waiting for transfers between devices  19.6 us (20%)
  starting transfers between devices  17 us (17%)
  local copies, waits for them, and re-layouts  3.23 us (3%)
  other arithmetic  2.73 us (3%)
  between operations  1.41 us (1%)
    all_to_all x1, blocking collectives, body(): lax.all_to_all(jnp.broadcast_to(mom[None], (strips, *mom.shape)), 'strip'...  24 us
    pallas_call x1, Pallas kernels, apply(): pl.pallas_call(apply_kernel, out_shape=jax.ShapeDtypeStruct((ROWS, COLS),...  21.1 us
    all_to_all x1, waiting for transfers between devices, body(): lax.all_to_all(outgoing, ('ccd', 'strip'), split_axis=0, concat_axis=0, t...  18.8 us
    all_to_all x1, starting transfers between devices, body(): lax.all_to_all(outgoing, ('ccd', 'strip'), split_axis=0, concat_axis=0, t...  11.2 us
    pallas_call x1, Pallas kernels, fit(): pl.pallas_call(fit_kernel, out_shape=(jax.ShapeDtypeStruct((ROWS * 32, CO...  8.97 us
    ppermute x1, starting transfers between devices, body(): above = lax.ppermute(own, 'strip', [(i, i + 1) for i in range(strips - 1)])  4.55 us
  transfers between devices with their start and end apart: 3, of which 2 were waited for; matrix products, arithmetic and copies ran while one was open for 1% of the time, Pallas kernels for 0%

commit v1 on v0

--- a/solution.py
+++ b/solution.py
@@ -183,10 +183,7 @@
 def apply_kernel(scal, moms, e_ref, sci, upow, out, mat, fx):
     order = scal[2]
     first_row = scal[1]
-    total = moms[0]
-    for i in range(1, moms.shape[0]):
-        total = total + moms[i]
-    units = [total[32 * i : 32 * i + 32] for i in range(4)]
+    units = [moms[32 * i : 32 * i + 32] for i in range(4)]
     lane = lax.broadcasted_iota(jnp.int32, (1, TC), 1)
     row = lax.broadcasted_iota(jnp.int32, (32, 1), 0)
     degree = lambda q: 0 if q == 0 else (1 if q < 3 else 2)
@@ -278,6 +275,150 @@
     out[...] = sci[...] - (t0 + u * (t1 + u * t2))
 
 
+MESH = pl.DeviceIdType.MESH
+
+
+def tiles_kernel(ccds, strips, pick, owner, store, own, above, below, sent, got, edge, send, recv, esend, erecv):
+    ccd = lax.axis_index("ccd")
+    strip = lax.axis_index("strip")
+    count = ccds * strips
+    me = ccd * strips + strip
+    barrier = pltpu.get_barrier_semaphore()
+
+    def peer(k):
+        return lax.rem(ccd + k // strips, ccds), lax.rem(strip + lax.rem(k, strips), strips)
+
+    def greet(k, carry):
+        pl.semaphore_signal(barrier, inc=1, device_id=peer(k), device_id_type=MESH)
+        return carry
+
+    lax.fori_loop(1, count, greet, 0)
+
+    def choose(d, carry):
+        sent[d] = store[pick[d]]
+        return carry
+
+    lax.fori_loop(0, count, choose, 0)
+    got[me] = sent[me]
+    pl.semaphore_wait(barrier, count - 1)
+
+    def push(k, carry):
+        to = peer(k)
+        pltpu.make_async_remote_copy(
+            src_ref=sent.at[to[0] * strips + to[1]],
+            dst_ref=got.at[me],
+            send_sem=send,
+            recv_sem=recv,
+            device_id=to,
+            device_id_type=MESH,
+        ).start()
+        return carry
+
+    lax.fori_loop(1, count, push, 0)
+    rest = got.at[pl.ds(0, count - 1)]
+    pltpu.make_async_copy(rest, rest, recv).wait()
+    for t in range(own.shape[0]):
+        own[t] = got[owner[t]]
+
+    def edge_copy(way):
+        return pltpu.make_async_remote_copy(
+            src_ref=own,
+            dst_ref=edge.at[way],
+            send_sem=esend.at[way],
+            recv_sem=erecv.at[way],
+            device_id=(ccd, lax.rem(strip + (1 if way == 0 else strips - 1), strips)),
+            device_id_type=MESH,
+        )
+
+    for way in range(2):
+        edge_copy(way).start()
+    for way in range(2):
+        edge_copy(way).wait()
+    above[...] = jnp.where(strip > 0, edge[0], 0.0)
+    below[...] = jnp.where(strip < strips - 1, edge[1], 0.0)
+    pltpu.make_async_copy(rest, rest, send).wait()
+
+
+def exchange(pick, owner, store, ccds, strips):
+    tiles = jax.ShapeDtypeStruct((owner.shape[0], *store.shape[1:]), F32)
+    count = ccds * strips
+    return pl.pallas_call(
+        lambda *refs: tiles_kernel(ccds, strips, *refs),
+        out_shape=(tiles, tiles, tiles),
+        in_specs=[SM, SM, VM],
+        out_specs=(VM, VM, VM),
+        scratch_shapes=[
+            pltpu.VMEM((count, *store.shape[1:]), F32),
+            pltpu.VMEM((count, *store.shape[1:]), F32),
+            pltpu.VMEM((2, *tiles.shape), F32),
+            pltpu.SemaphoreType.DMA,
+            pltpu.SemaphoreType.DMA,
+            pltpu.SemaphoreType.DMA((2,)),
+            pltpu.SemaphoreType.DMA((2,)),
+        ],
+        compiler_params=pltpu.CompilerParams(
+            collective_id=0, has_side_effects=True, vmem_limit_bytes=LIMIT
+        ),
+        name="tiles",
+    )(pick, owner, store)
+
+
+def total_kernel(strips, mom, out, got, part, all_parts, s1, r1, s2, r2):
+    ccd = lax.axis_index("ccd")
+    strip = lax.axis_index("strip")
+    barrier = pltpu.get_barrier_semaphore()
+    peers = [(ccd, lax.rem(strip + k, strips)) for k in range(1, strips)]
+    for to in peers:
+        pl.semaphore_signal(barrier, inc=1, device_id=to, device_id_type=MESH)
+    pl.semaphore_wait(barrier, strips - 1)
+    for to in peers:
+        pltpu.make_async_remote_copy(
+            src_ref=mom.at[to[1]],
+            dst_ref=got.at[strip],
+            send_sem=s1,
+            recv_sem=r1,
+            device_id=to,
+            device_id_type=MESH,
+        ).start()
+    got[strip] = mom[strip]
+    rest = got.at[pl.ds(0, strips - 1)]
+    pltpu.make_async_copy(rest, rest, r1).wait()
+    total = got[0]
+    for i in range(1, strips):
+        total = total + got[i]
+    part[...] = total
+    for to in peers:
+        pltpu.make_async_remote_copy(
+            src_ref=part,
+            dst_ref=all_parts.at[strip],
+            send_sem=s2,
+            recv_sem=r2,
+            device_id=to,
+            device_id_type=MESH,
+        ).start()
+    all_parts[strip] = total
+    pltpu.make_async_copy(rest, rest, s1).wait()
+    pltpu.make_async_copy(rest, rest, s2).wait()
+    pltpu.make_async_copy(rest, rest, r2).wait()
+    out[...] = all_parts[...]
+
+
+def sum_over_strips(mom, strips):
+    rows = mom.shape[0] // strips
+    blocks = mom.reshape(strips, rows, TC)
+    buffer = pltpu.VMEM(blocks.shape, F32)
+    total = pl.pallas_call(
+        lambda *refs: total_kernel(strips, *refs),
+        out_shape=jax.ShapeDtypeStruct(blocks.shape, F32),
+        in_specs=[VM],
+        out_specs=VM,
+        scratch_shapes=[buffer, pltpu.VMEM((rows, TC), F32), buffer] + [pltpu.SemaphoreType.DMA] * 4,
+        compiler_params=pltpu.CompilerParams(collective_id=1, has_side_effects=True),
+        name="total",
+    )(blocks)
+    return total.reshape(mom.shape)
+
+
 VM = pl.BlockSpec(memory_space=pltpu.VMEM)
 SM = pl.BlockSpec(memory_space=pltpu.SMEM)
 LIMIT = 60 * 1024 * 1024
@@ -323,18 +464,12 @@
     strip = lax.axis_index("strip")
     me = lax.axis_index("ccd") * strips + strip
     pick = jnp.sum(jnp.where(tile_source == me, tile_slot, 0), axis=1)
-    outgoing = jnp.take(tile_store, pick, axis=0)
-    arrived = lax.all_to_all(outgoing, ("ccd", "strip"), split_axis=0, concat_axis=0, tiled=True)
     owner = lax.dynamic_index_in_dim(tile_source, me, 0, keepdims=False)
-    own = jnp.take(arrived, owner, axis=0)
-    above = lax.ppermute(own, "strip", [(i, i + 1) for i in range(strips - 1)])
-    below = lax.ppermute(own, "strip", [(i + 1, i) for i in range(strips - 1)])
+    own, above, below = exchange(pick, owner, tile_store, lax.axis_size("ccd"), strips)
     scal = jnp.stack([shift_cols[0], strip * ROWS, spatial_order[0]]).astype(jnp.int32)
     e, mom = fit(scal, own, above, below, science)
-    moms = lax.all_to_all(
-        jnp.broadcast_to(mom[None], (strips, *mom.shape)), "strip", 0, 0, tiled=True
-    )
-    return apply(scal, moms, e, science)
+    total = sum_over_strips(mom, strips)
+    return apply(scal, total, e, science)
 
 
 def solution(mesh):

time: 98.5 us -> 84.3 us (0.86)
  Pallas kernels: 30.1 us -> 79.3 us
  blocking collectives: 24 us -> 0 us
  waiting for transfers between devices: 19.6 us -> 0 us
  starting transfers between devices: 17 us -> 0 us
  local copies, waits for them, and re-layouts: 3.23 us -> 1.48 us
    pallas_call x0 -> x2, Pallas kernels: none -> 49.4 us  [the longest x1 35.8 us: exchange(): pl.pallas_call(lambda *refs: tiles_kernel(ccds, strips, *refs), out_shape...]
    all_to_all x1 -> x0, blocking collectives: 24 us -> none  [body(): lax.all_to_all(jnp.broadcast_to(mom[None], (strips, *mom.shape)), 'strip'...]
    all_to_all x1 -> x0, waiting for transfers between devices: 18.8 us -> none  [body(): lax.all_to_all(outgoing, ('ccd', 'strip'), split_axis=0, concat_axis=0, t...]
    all_to_all x1 -> x0, starting transfers between devices: 11.2 us -> none  [body(): lax.all_to_all(outgoing, ('ccd', 'strip'), split_axis=0, concat_axis=0, t...]
    ppermute x2 -> x0, starting transfers between devices: 5.85 us -> none  [the longest x1 4.55 us: body(): above = lax.ppermute(own, 'strip', [(i, i + 1) for i in range(strips - 1)])]
    gather x2 -> x0, local copies, waits for them, and re-layouts: 1.33 us -> none  [the longest x1 0.76 us: body(): outgoing = jnp.take(tile_store, pick, axis=0)]
    dynamic_slice x1, local copies, waits for them, and re-layouts: 0.18 us -> 1.48 us  [body(): owner = lax.dynamic_index_in_dim(tile_source, me, 0, keepdims=False)]
    select_n x4 -> x0, other arithmetic: 1.27 us -> none  [the longest x2 1.17 us: body(): outgoing = jnp.take(tile_store, pick, axis=0)]
  transfers between devices with their start and end apart: 3 -> 0, of which waited for: 2 -> 0; matrix products, arithmetic and copies ran while one was open for 1% -> 0% of each run, Pallas kernels for 0% -> 0%
where the time goes in v1:
time: 84.3 us; the launch traced here: 83.9 us
  Pallas kernels  79.3 us (94%)
  other arithmetic  1.86 us (2%)
  local copies, waits for them, and re-layouts  1.48 us (2%)
  between operations  1.31 us (2%)
    pallas_call x1, Pallas kernels, exchange(): pl.pallas_call(lambda *refs: tiles_kernel(ccds, strips, *refs), out_shape...  35.8 us
    pallas_call x1, Pallas kernels, apply(): pl.pallas_call(apply_kernel, out_shape=jax.ShapeDtypeStruct((ROWS, COLS),...  20.9 us
    pallas_call x1, Pallas kernels, sum_over_strips(): pl.pallas_call(lambda *refs: total_kernel(strips, *refs), out_shape=jax.S...  13.6 us
    pallas_call x1, Pallas kernels, fit(): pl.pallas_call(fit_kernel, out_shape=(jax.ShapeDtypeStruct((ROWS * 32, CO...  9.01 us

profile of v1, /device:TPU:0, one launch (start us, length us, event | category | flops | bytes accessed | tf_op | source)
XLA Modules:
  0.0 83.9 jit_solution(6344779844689170466)
XLA Ops:
  1.3 0.6 pad_add_fusion.scal
  1.9 1.5 %dynamic-slice_reduce_fusion.refs_1_ = s32[18]{0:T(128)} fusion(s32[128,18]{0,1:T(8,128)} %param.12, s32[]{:T(128)S(6)} %select_n.9), kind=kLoop, calls=%fused_computation | loop fusion | bytes 148 | tf_op jit(solution)/shard_map/jit(dynamic_index_in_dim)/dynamic_slice | solution.py:467
  3.4 1.2 %select_reduce_fusion.refs_0_ = s32[128]{0:T(128)} fusion(s32[128,18]{0,1:T(8,128)} %param.13, s32[128,18]{0,1:T(8,128)} %param.12, s32[]{:T(128)S(6)} %add.7), kind=kLoop, calls=%fused_computation.1 | loop fusion | flops 6784 | bytes 18948 | tf_op jit(solution)/shard_map/reduce_sum | solution.py:466
  4.6 35.8 %tiles.1 = (f32[18,16,128]{2,1,0:T(8,128)}, f32[18,16,128]{2,1,0:T(8,128)}, f32[18,16,128]{2,1,0:T(8,128)}) custom-call(s32[128]{0:T(128)} %select_reduce_fusion.refs_0_, s32[18]{0:T(128)} %dynamic-slice_reduce_fusion.refs_1_, f32[18,16,128]{2,1,0:T(8,128)} %refs_2_.1), custom_call_target="tpu_custom_call" | custom-call | tf_op jit(solution)/shard_map/tiles/pallas_call | solution.py:345
  40.5 9.0 %fit.1 = (bf16[512,2048]{1,0:T(8,128)(2,1)}, f32[128,128]{1,0:T(8,128)}) custom-call(s32[3]{0:T(128)} %pad_add_fusion.scal, f32[18,16,128]{2,1,0:T(8,128)} %get-tuple-element.10.own, f32[18,16,128]{2,1,0:T(8,128)} %get-tuple-element.11.above, f32[18,16,128]{2,1,0:T(8,128)} %get-tuple-element.12.below, f32[16,2048]{1,0:T(8,128)} %sci.3, ...), custom_call_target="tpu_custom_call" | custom-call | tf_op jit(solution)/shard_map/fit/pallas_call | solution.py:431
  49.5 13.6 %total.1 = f32[16,8,128]{2,1,0:T(8,128)} custom-call(f32[16,8,128]{2,1,0:T(8,128)} %bitcast.4), custom_call_target="tpu_custom_call" | custom-call | tf_op jit(solution)/shard_map/total/pallas_call | solution.py:410
  63.1 20.9 %apply.1 = f32[16,2048]{1,0:T(8,128)} custom-call(s32[3]{0:T(128)} %pad_add_fusion.scal, f32[128,128]{1,0:T(8,128)} %bitcast.3, bf16[512,2048]{1,0:T(8,128)(2,1)} %get-tuple-element.14.e_ref, f32[16,2048]{1,0:T(8,128)} %sci.3, f32[8,2048]{1,0:T(8,128)} %constant.29.clone.upow), custom_call_target="tpu_custom_call" | custom-call | tf_op jit(solution)/shard_map/apply/pallas_call | solution.py:451

commit v2 on v1

--- a/solution.py
+++ b/solution.py
@@ -180,6 +180,91 @@
     return {(4, 0): (2, 3), (0, 3): (3, 0), (1, 3): (3, 1), (0, 4): (3, 2)}[(k, m)]
 
 
+def inverse2(m):
+    (a, b), (c, d) = m
+    r = 1.0 / (a * d - b * c)
+    return (d * r, -b * r), (-c * r, a * r)
+
+
+def times2(x, y):
+    return tuple(tuple(x[i][0] * y[0][j] + x[i][1] * y[1][j] for j in range(2)) for i in range(2))
+
+
+def plus2(x, y, sign):
+    return tuple(tuple(x[i][j] + sign * y[i][j] for j in range(2)) for i in range(2))
+
+
+def inverse4(p):
+    part = lambda i, j: tuple(tuple(p[2 * i + a][2 * j + b] for b in range(2)) for a in range(2))
+    head = inverse2(part(0, 0))
+    x = times2(head, part(0, 1))
+    y = times2(part(1, 0), head)
+    tail = inverse2(plus2(part(1, 1), times2(part(1, 0), x), -1.0))
+    xt = times2(x, tail)
+    low = times2(tail, y)
+    top = plus2(head, times2(xt, y), 1.0)
+    return [
+        [top[i][j] if i < 2 and j < 2 else tail[i - 2][j - 2] if i > 1 and j > 1
+         else -xt[i][j - 2] if i < 2 else -low[i - 2][j] for j in range(4)]
+        for i in range(4)
+    ]
+
+
+def sweep_panel(mat, fx, q, lane):
+    t = q // 4
+    top = 32 * q
+    base = 32 * (q % 4)
+    sub = lax.broadcasted_iota(jnp.int32, (8, TC), 0)
+    tiles = [[mat[top + 8 * i : top + 8 * i + 8, TC * h : TC * h + TC] for h in range(2)] for i in range(4)]
+    for k in range(0, 28, 4):
+        i0, s0, l0 = k // 8, k % 8, base + k
+        cols = [
+            [jnp.broadcast_to(tiles[i][t][:, l0 + j : l0 + j + 1], (8, TC)) for j in range(4)]
+            for i in range(4)
+        ]
+        p = [[jnp.broadcast_to(cols[i0][j][s0 + i : s0 + i + 1], (8, TC)) for j in range(4)] for i in range(4)]
+        w = inverse4(p)
+        in_lane = (lane >= l0) & (lane < l0 + 4)
+        in_row = (sub >= s0) & (sub < s0 + 4)
+        rows = []
+        for h in range(2):
+            r = [jnp.broadcast_to(tiles[i0][h][s0 + j : s0 + j + 1], (8, TC)) for j in range(4)]
+            if h == t:
+                r = [jnp.where(in_lane, jnp.where(lane == l0 + j, 1.0, 0.0), r[j]) for j in range(4)]
+            rows.append([
+                (w[m][0] * r[0] + w[m][1] * r[1]) + (w[m][2] * r[2] + w[m][3] * r[3]) for m in range(4)
+            ])
+        for i in range(4):
+            c = cols[i]
+            if i == i0:
+                c = [jnp.where(in_row, jnp.where(sub == s0 + j, -1.0, 0.0), c[j]) for j in range(4)]
+            for h in range(2):
+                old = tiles[i][h]
+                if h == t:
+                    old = jnp.where(in_lane, 0.0, old)
+                if i == i0:
+                    old = jnp.where(in_row, 0.0, old)
+                u = rows[h]
+                tiles[i][h] = old - ((c[0] * u[0] + c[1] * u[1]) + (c[2] * u[2] + c[3] * u[3]))
+    fx[...] = jnp.zeros_like(fx)
+    inside = (lane >= base) & (lane < base + 28)
+    for i in range(4):
+        for h in range(2):
+            f = tiles[i][h]
+            if h == t:
+                f = jnp.where(inside, -f, f)
+            if i == 3:
+                f = jnp.where(sub < 4, f, 0.0)
+            fx[base + 8 * i : base + 8 * i + 8, TC * h : TC * h + TC] = f
+    rest = mat[top + 32 : 200, TC * t : TC * t + TC]
+    change = jnp.dot(rest, fx[...], preferred_element_type=F32, precision=lax.Precision.HIGHEST)
+    for h in range(2):
+        old = mat[top + 32 : 200, TC * h : TC * h + TC]
+        if h == t:
+            old = jnp.where(inside, 0.0, old)
+        mat[top + 32 : 200, TC * h : TC * h + TC] = old - change[:, TC * h : TC * h + TC]
+
+
 def apply_kernel(scal, moms, e_ref, sci, upow, out, mat, fx):
     order = scal[2]
     first_row = scal[1]
@@ -212,41 +297,8 @@
             mat[32 * q : 32 * q + 32, TC * t : TC * t + TC] = block
             if q == 0:
                 mat[192:200, TC * t : TC * t + TC] = jnp.where(col_active(t), block[24:32], 0.0)
-    wide = lax.broadcasted_iota(jnp.int32, (1, 2 * TC), 1)
     for q in range(6):
-        t = q // 4
-        top = 32 * q
-        base = 32 * (q % 4)
-
-        def sweep(b, carry, t=t, top=top, base=base):
-            panel = mat[top : top + 32, :]
-            prow = mat[pl.ds(top + b, 1), :]
-            at = lane == base + b
-            col = jnp.sum(
-                jnp.where(at, panel[:, TC * t : TC * t + TC], 0.0), axis=1, keepdims=True
-            )
-            d = jnp.sum(jnp.where(at, prow[:, TC * t : TC * t + TC], 0.0), axis=1, keepdims=True)
-            inv = 1.0 / d
-            here = row == b
-            g = jnp.where(here, -1.0, col) * inv
-            atw = wide == TC * t + base + b
-            mat[top : top + 32, :] = jnp.where(atw | here, 0.0, panel) - g * jnp.where(atw, 1.0, prow)
-            return carry
-
-        lax.fori_loop(0, 28, sweep, 0)
-        panel = mat[top : top + 32, :]
-        local = wide - (TC * t + base)
-        inside = (local >= 0) & (local < 28)
-        f = jnp.where(row < 28, jnp.where(inside, -panel, panel), 0.0)
-        fx[...] = jnp.zeros_like(fx)
-        fx[base : base + 32, :] = f
-        rest = mat[top + 32 : 200, :]
-        mat[top + 32 : 200, :] = jnp.where(inside, 0.0, rest) - jnp.dot(
-            rest[:, TC * t : TC * t + TC],
-            fx[...],
-            preferred_element_type=F32,
-            precision=lax.Precision.HIGHEST,
-        )
+        sweep_panel(mat, fx, q, lane)
     coef = []
     for q in range(6):
         z = mat[192:200, TC * (q // 4) : TC * (q // 4) + TC]

time: 84.3 us -> 75.6 us (0.90)
  Pallas kernels: 79.3 us -> 70.6 us
    pallas_call x1, Pallas kernels: 20.9 us -> 12.2 us  [apply(): pl.pallas_call(apply_kernel, out_shape=jax.ShapeDtypeStruct((ROWS, COLS),...]
where the time goes in v2:
time: 75.6 us; the launch traced here: 75.3 us
  Pallas kernels  70.6 us (93%)
  other arithmetic  1.86 us (2%)
  local copies, waits for them, and re-layouts  1.48 us (2%)
  between operations  1.31 us (2%)
    pallas_call x1, Pallas kernels, exchange(): pl.pallas_call(lambda *refs: tiles_kernel(ccds, strips, *refs), out_shape...  35.8 us
    pallas_call x1, Pallas kernels, sum_over_strips(): pl.pallas_call(lambda *refs: total_kernel(strips, *refs), out_shape=jax.S...  13.6 us
    pallas_call x1, Pallas kernels, apply(): pl.pallas_call(apply_kernel, out_shape=jax.ShapeDtypeStruct((ROWS, COLS),...  12.2 us
    pallas_call x1, Pallas kernels, fit(): pl.pallas_call(fit_kernel, out_shape=(jax.ShapeDtypeStruct((ROWS * 32, CO...  9.01 us

profile of v2, /device:TPU:0, one launch (start us, length us, event | category | flops | bytes accessed | tf_op | source)
XLA Modules:
  0.0 75.3 jit_solution(13023247995455366180)
XLA Ops:
  1.3 0.6 pad_add_fusion.scal
  1.9 1.5 %dynamic-slice_reduce_fusion.refs_1_ = s32[18]{0:T(128)} fusion(s32[128,18]{0,1:T(8,128)} %param.12, s32[]{:T(128)S(6)} %select_n.9), kind=kLoop, calls=%fused_computation | loop fusion | bytes 148 | tf_op jit(solution)/shard_map/jit(dynamic_index_in_dim)/dynamic_slice | solution.py:519
  3.4 1.2 %select_reduce_fusion.refs_0_ = s32[128]{0:T(128)} fusion(s32[128,18]{0,1:T(8,128)} %param.13, s32[128,18]{0,1:T(8,128)} %param.12, s32[]{:T(128)S(6)} %add.7), kind=kLoop, calls=%fused_computation.1 | loop fusion | flops 6784 | bytes 18948 | tf_op jit(solution)/shard_map/reduce_sum | solution.py:518
  4.6 35.8 %tiles.1 = (f32[18,16,128]{2,1,0:T(8,128)}, f32[18,16,128]{2,1,0:T(8,128)}, f32[18,16,128]{2,1,0:T(8,128)}) custom-call(s32[128]{0:T(128)} %select_reduce_fusion.refs_0_, s32[18]{0:T(128)} %dynamic-slice_reduce_fusion.refs_1_, f32[18,16,128]{2,1,0:T(8,128)} %refs_2_.1), custom_call_target="tpu_custom_call" | custom-call | tf_op jit(solution)/shard_map/tiles/pallas_call | solution.py:397
  40.5 9.0 %fit.1 = (bf16[512,2048]{1,0:T(8,128)(2,1)}, f32[128,128]{1,0:T(8,128)}) custom-call(s32[3]{0:T(128)} %pad_add_fusion.scal, f32[18,16,128]{2,1,0:T(8,128)} %get-tuple-element.10.own, f32[18,16,128]{2,1,0:T(8,128)} %get-tuple-element.11.above, f32[18,16,128]{2,1,0:T(8,128)} %get-tuple-element.12.below, f32[16,2048]{1,0:T(8,128)} %sci.3, ...), custom_call_target="tpu_custom_call" | custom-call | tf_op jit(solution)/shard_map/fit/pallas_call | solution.py:483
  49.5 13.6 %total.1 = f32[16,8,128]{2,1,0:T(8,128)} custom-call(f32[16,8,128]{2,1,0:T(8,128)} %bitcast.4), custom_call_target="tpu_custom_call" | custom-call | tf_op jit(solution)/shard_map/total/pallas_call | solution.py:462
  63.1 12.2 %apply.1 = f32[16,2048]{1,0:T(8,128)} custom-call(s32[3]{0:T(128)} %pad_add_fusion.scal, f32[128,128]{1,0:T(8,128)} %bitcast.3, bf16[512,2048]{1,0:T(8,128)(2,1)} %get-tuple-element.14.e_ref, f32[16,2048]{1,0:T(8,128)} %sci.3, f32[8,2048]{1,0:T(8,128)} %constant.29.clone.upow), custom_call_target="tpu_custom_call" | custom-call | tf_op jit(solution)/shard_map/apply/pallas_call | solution.py:503

commit v3 on v2

--- a/solution.py
+++ b/solution.py
@@ -87,17 +87,15 @@
     return np.stack([u, u * u] + [np.zeros_like(u)] * 6)
 
 
-def fit_kernel(scal, own, above, below, sci, band, va, vb, upow, e_out, mom_out, rolled, hs, acc):
-    shift = scal[0]
-    first_row = scal[1]
+def fit_stage(shift, first_row, own, above, below, sci, band, va, vb, upow, e_out, mom_out, rolled, hs, acc):
     start = CM + shift - H
     tile = lax.shift_right_logical(start, 7)
     rem = lax.bitwise_and(start, 127)
     count = own.shape[0]
     row16 = lax.broadcasted_iota(jnp.int32, (1, 16, TC), 1)
     row8 = lax.broadcasted_iota(jnp.int32, (1, 8, TC), 1)
-    a = pltpu.roll(above[...], H, 1)
-    b = pltpu.roll(below[...], H, 1)
+    a = pltpu.roll(above, H, 1)
+    b = pltpu.roll(below, H, 1)
     mid = jnp.where(row16 < H, a, b)
     end = jnp.where(row8 < 6, b[:, :8], jnp.where(row8 == 6, 1.0, 0.0))
     x = jnp.concatenate([own[...], mid, end], axis=1)
@@ -169,7 +167,8 @@
         jnp.where(lane < 64, acc[3, 0:32], pltpu.roll(acc[4, 0:32], 64, 1)),
     )
     for i, unit in enumerate(units):
-        mom_out[32 * i : 32 * i + 32] = unit
+        for j in range(4):
+            mom_out[4 * i + j] = unit[8 * j : 8 * j + 8]
 
 
 def unit_of(k, m):
@@ -265,10 +264,8 @@
         mat[top + 32 : 200, TC * h : TC * h + TC] = old - change[:, TC * h : TC * h + TC]
 
 
-def apply_kernel(scal, moms, e_ref, sci, upow, out, mat, fx):
-    order = scal[2]
-    first_row = scal[1]
-    units = [moms[32 * i : 32 * i + 32] for i in range(4)]
+def apply_stage(order, first_row, moms, e_ref, sci, upow, out, mat, fx):
+    units = [jnp.concatenate([moms[4 * i + j] for j in range(4)], axis=0) for i in range(4)]
     lane = lax.broadcasted_iota(jnp.int32, (1, TC), 1)
     row = lax.broadcasted_iota(jnp.int32, (32, 1), 0)
     degree = lambda q: 0 if q == 0 else (1 if q < 3 else 2)
@@ -330,12 +327,22 @@
 MESH = pl.DeviceIdType.MESH
 
 
-def tiles_kernel(ccds, strips, pick, owner, store, own, above, below, sent, got, edge, send, recv, esend, erecv):
+def whole_kernel(
+    ccds, strips, pick, owner, shift, order, store, sci_h, band_h, va_h, vb_h, upow_h, out,
+    sent, got, own, edge, sci, band, va, vb, upow, e, rolled, hs, acc, mom, parts, part, totals, mat, fx,
+    local, send, recv, esend, erecv, s1, r1, s2, r2,
+):
     ccd = lax.axis_index("ccd")
     strip = lax.axis_index("strip")
     count = ccds * strips
     me = ccd * strips + strip
     barrier = pltpu.get_barrier_semaphore()
+    loads = [
+        pltpu.make_async_copy(h, v, local.at[i])
+        for i, (h, v) in enumerate(
+            ((band_h, band), (va_h, va), (vb_h, vb), (upow_h, upow), (sci_h, sci))
+        )
+    ]
 
     def peer(k):
         return lax.rem(ccd + k // strips, ccds), lax.rem(strip + lax.rem(k, strips), strips)
@@ -345,12 +352,14 @@
         return carry
 
     lax.fori_loop(1, count, greet, 0)
+    for load in loads:
+        load.start()
 
     def choose(d, carry):
         sent[d] = store[pick[d]]
         return carry
 
-    lax.fori_loop(0, count, choose, 0)
+    lax.fori_loop(0, count, choose, 0, unroll=8)
     got[me] = sent[me]
     pl.semaphore_wait(barrier, count - 1)
 
@@ -371,9 +380,8 @@
     pltpu.make_async_copy(rest, rest, recv).wait()
     for t in range(own.shape[0]):
         own[t] = got[owner[t]]
-
-    def edge_copy(way):
-        return pltpu.make_async_remote_copy(
+    edges = [
+        pltpu.make_async_remote_copy(
             src_ref=own,
             dst_ref=edge.at[way],
             send_sem=esend.at[way],
@@ -381,147 +389,111 @@
             device_id=(ccd, lax.rem(strip + (1 if way == 0 else strips - 1), strips)),
             device_id_type=MESH,
         )
-
-    for way in range(2):
-        edge_copy(way).start()
-    for way in range(2):
-        edge_copy(way).wait()
-    above[...] = jnp.where(strip > 0, edge[0], 0.0)
-    below[...] = jnp.where(strip < strips - 1, edge[1], 0.0)
-    pltpu.make_async_copy(rest, rest, send).wait()
-
-
-def exchange(pick, owner, store, ccds, strips):
-    tiles = jax.ShapeDtypeStruct((owner.shape[0], *store.shape[1:]), F32)
-    count = ccds * strips
-    return pl.pallas_call(
-        lambda *refs: tiles_kernel(ccds, strips, *refs),
-        out_shape=(tiles, tiles, tiles),
-        in_specs=[SM, SM, VM],
-        out_specs=(VM, VM, VM),
-        scratch_shapes=[
-            pltpu.VMEM((count, *store.shape[1:]), F32),
-            pltpu.VMEM((count, *store.shape[1:]), F32),
-            pltpu.VMEM((2, *tiles.shape), F32),
-            pltpu.SemaphoreType.DMA,
-            pltpu.SemaphoreType.DMA,
-            pltpu.SemaphoreType.DMA((2,)),
-            pltpu.SemaphoreType.DMA((2,)),
-        ],
-        compiler_params=pltpu.CompilerParams(
-            collective_id=0, has_side_effects=True, vmem_limit_bytes=LIMIT
-        ),
-        name="tiles",
-    )(pick, owner, store)
-
-
-def total_kernel(strips, mom, out, got, part, all_parts, s1, r1, s2, r2):
-    ccd = lax.axis_index("ccd")
-    strip = lax.axis_index("strip")
-    barrier = pltpu.get_barrier_semaphore()
+        for way in range(2)
+    ]
+    for copy in edges:
+        copy.start()
+    for load in loads:
+        load.wait()
+    for copy in edges:
+        copy.wait()
+    above = jnp.where(strip > 0, edge[0], 0.0)
+    below = jnp.where(strip < strips - 1, edge[1], 0.0)
+    first_row = strip * ROWS
+    fit_stage(shift[0], first_row, own, above, below, sci, band, va, vb, upow, e, mom, rolled, hs, acc)
     peers = [(ccd, lax.rem(strip + k, strips)) for k in range(1, strips)]
-    for to in peers:
-        pl.semaphore_signal(barrier, inc=1, device_id=to, device_id_type=MESH)
-    pl.semaphore_wait(barrier, strips - 1)
     for to in peers:
         pltpu.make_async_remote_copy(
             src_ref=mom.at[to[1]],
-            dst_ref=got.at[strip],
+            dst_ref=parts.at[strip],
             send_sem=s1,
             recv_sem=r1,
             device_id=to,
             device_id_type=MESH,
         ).start()
-    got[strip] = mom[strip]
-    rest = got.at[pl.ds(0, strips - 1)]
-    pltpu.make_async_copy(rest, rest, r1).wait()
-    total = got[0]
+    parts[strip] = mom[strip]
+    few = parts.at[pl.ds(0, strips - 1)]
+    pltpu.make_async_copy(few, few, r1).wait()
+    total = parts[0]
     for i in range(1, strips):
-        total = total + got[i]
+        total = total + parts[i]
     part[...] = total
     for to in peers:
         pltpu.make_async_remote_copy(
             src_ref=part,
-            dst_ref=all_parts.at[strip],
+            dst_ref=totals.at[strip],
             send_sem=s2,
             recv_sem=r2,
             device_id=to,
             device_id_type=MESH,
         ).start()
-    all_parts[strip] = total
-    pltpu.make_async_copy(rest, rest, s1).wait()
-    pltpu.make_async_copy(rest, rest, s2).wait()
-    pltpu.make_async_copy(rest, rest, r2).wait()
-    out[...] = all_parts[...]
-
-
-def sum_over_strips(mom, strips):
-    rows = mom.shape[0] // strips
-    blocks = mom.reshape(strips, rows, TC)
-    buffer = pltpu.VMEM(blocks.shape, F32)
-    total = pl.pallas_call(
-        lambda *refs: total_kernel(strips, *refs),
-        out_shape=jax.ShapeDtypeStruct(blocks.shape, F32),
-        in_specs=[VM],
-        out_specs=VM,
-        scratch_shapes=[buffer, pltpu.VMEM((rows, TC), F32), buffer] + [pltpu.SemaphoreType.DMA] * 4,
-        compiler_params=pltpu.CompilerParams(collective_id=1, has_side_effects=True),
-        name="total",
-    )(blocks)
-    return total.reshape(mom.shape)
+    totals[strip] = total
+    pltpu.make_async_copy(few, few, r2).wait()
+    apply_stage(order[0], first_row, totals, e, sci, upow, out, mat, fx)
+    pltpu.make_async_copy(rest, rest, send).wait()
+    pltpu.make_async_copy(few, few, s1).wait()
+    pltpu.make_async_copy(few, few, s2).wait()
 
 
 VM = pl.BlockSpec(memory_space=pltpu.VMEM)
 SM = pl.BlockSpec(memory_space=pltpu.SMEM)
+ANY = pl.BlockSpec(memory_space=pl.ANY)
 LIMIT = 60 * 1024 * 1024
 
 
-def fit(scal, own, above, below, sci):
-    band = jnp.asarray(band_matrix())
-    va, vb = (jnp.asarray(m) for m in vertical_matrices())
-    upow = jnp.asarray(column_powers())
+def whole(pick, owner, shift, order, store, sci, ccds, strips):
+    count = ccds * strips
+    tiles = (owner.shape[0], *store.shape[1:])
+    tables = [band_matrix(), *vertical_matrices(), column_powers()]
+    blocks = pltpu.VMEM((strips, 128 // strips, TC), F32)
+    dma = pltpu.SemaphoreType.DMA
     return pl.pallas_call(
-        fit_kernel,
-        out_shape=(
-            jax.ShapeDtypeStruct((ROWS * 32, COLS), BF16),
-            jax.ShapeDtypeStruct((128, TC), F32),
-        ),
-        in_specs=[SM] + [VM] * 8,
-        out_specs=(VM, VM),
+        lambda *refs: whole_kernel(ccds, strips, *refs),
+        out_shape=jax.ShapeDtypeStruct((ROWS, COLS), F32),
+        in_specs=[SM] * 4 + [VM] + [ANY] * 5,
+        out_specs=VM,
         scratch_shapes=[
-            pltpu.VMEM((own.shape[0] + 1, SLOTS, TC), F32),
+            pltpu.VMEM((count, *store.shape[1:]), F32),
+            pltpu.VMEM((count, *store.shape[1:]), F32),
+            pltpu.VMEM(tiles, F32),
+            pltpu.VMEM((2, *tiles), F32),
+            pltpu.VMEM((ROWS, COLS), F32),
+            *[pltpu.VMEM(x.shape, x.dtype) for x in tables],
+            pltpu.VMEM((ROWS * 32, COLS), BF16),
+            pltpu.VMEM((tiles[0] + 1, SLOTS, TC), F32),
             pltpu.VMEM((440, COLS), F32),
             pltpu.VMEM((5, 64, TC), F32),
+            blocks,
+            blocks,
+            pltpu.VMEM((128 // strips, TC), F32),
+            blocks,
+            pltpu.VMEM((200, 2 * TC), F32),
+            pltpu.VMEM((TC, 2 * TC), F32),
+            dma((5,)),
+            dma,
+            dma,
+            dma((2,)),
+            dma((2,)),
+            dma,
+            dma,
+            dma,
+            dma,
         ],
-        compiler_params=pltpu.CompilerParams(vmem_limit_bytes=LIMIT),
-        name="fit",
-    )(scal, own, above, below, sci, band, va, vb, upow)
-
-
-def apply(scal, moms, e, sci):
-    upow = jnp.asarray(column_powers())
-    return pl.pallas_call(
-        apply_kernel,
-        out_shape=jax.ShapeDtypeStruct((ROWS, COLS), F32),
-        in_specs=[SM] + [VM] * 4,
-        out_specs=VM,
-        scratch_shapes=[pltpu.VMEM((200, 2 * TC), F32), pltpu.VMEM((TC, 2 * TC), F32)],
-        compiler_params=pltpu.CompilerParams(vmem_limit_bytes=LIMIT),
-        name="apply",
-    )(scal, moms, e, sci, upow)
+        compiler_params=pltpu.CompilerParams(
+            collective_id=0, has_side_effects=True, vmem_limit_bytes=LIMIT
+        ),
+        name="whole",
+    )(pick, owner, shift, order, store, sci, *[jnp.asarray(x) for x in tables])
 
 
 def body(tile_store, tile_source, tile_slot, shift_cols, spatial_order, science):
     strips = lax.axis_size("strip")
-    strip = lax.axis_index("strip")
-    me = lax.axis_index("ccd") * strips + strip
+    me = lax.axis_index("ccd") * strips + lax.axis_index("strip")
     pick = jnp.sum(jnp.where(tile_source == me, tile_slot, 0), axis=1)
     owner = lax.dynamic_index_in_dim(tile_source, me, 0, keepdims=False)
-    own, above, below = exchange(pick, owner, tile_store, lax.axis_size("ccd"), strips)
-    scal = jnp.stack([shift_cols[0], strip * ROWS, spatial_order[0]]).astype(jnp.int32)
-    e, mom = fit(scal, own, above, below, science)
-    total = sum_over_strips(mom, strips)
-    return apply(scal, total, e, science)
+    return whole(
+        pick, owner, shift_cols, spatial_order, tile_store, science, lax.axis_size("ccd"), strips
+    )
 
 
 def solution(mesh):

time: 75.6 us -> 67.3 us (0.89)
  Pallas kernels: 70.6 us -> 61.5 us
  local copies, waits for them, and re-layouts: 1.48 us -> 2.97 us
    pallas_call x4 -> x1, Pallas kernels: 70.6 us -> 61.5 us  [whole(): pl.pallas_call(lambda *refs: whole_kernel(ccds, strips, *refs), out_shape...]
    unnamed x0 -> x1, local copies, waits for them, and re-layouts: none -> 1.57 us
where the time goes in v3:
time: 67.3 us; the launch traced here: 67 us
  Pallas kernels  61.5 us (91%)
  local copies, waits for them, and re-layouts  2.97 us (4%)
  between operations  1.31 us (2%)
  other arithmetic  1.25 us (2%)
    pallas_call x1, Pallas kernels, whole(): pl.pallas_call(lambda *refs: whole_kernel(ccds, strips, *refs), out_shape...  61.5 us
    unnamed x1, local copies, waits for them, and re-layouts  1.57 us
    dynamic_slice x1, local copies, waits for them, and re-layouts, body(): owner = lax.dynamic_index_in_dim(tile_source, me, 0, keepdims=False)  1.4 us

profile of v3, /device:TPU:0, one launch (start us, length us, event | category | flops | bytes accessed | tf_op | source)
XLA Modules:
  0.0 67.0 jit_solution(8196091115709129737)
XLA Ops:
  1.3 1.4 %dynamic-slice_reduce_fusion.refs_1_ = s32[18]{0:T(128)} fusion(s32[128,18]{0,1:T(8,128)} %param.11, s32[]{:T(128)S(6)} %select_n.9), kind=kLoop, calls=%fused_computation | loop fusion | bytes 148 | tf_op jit(solution)/shard_map/jit(dynamic_index_in_dim)/dynamic_slice | solution.py:493
  2.7 1.2 %select_reduce_fusion.refs_0_ = s32[128]{0:T(128)} fusion(s32[128,18]{0,1:T(8,128)} %param.12, s32[128,18]{0,1:T(8,128)} %param.11, s32[]{:T(128)S(6)} %add.7), kind=kLoop, calls=%fused_computation.1 | loop fusion | flops 6784 | bytes 18948 | tf_op jit(solution)/shard_map/reduce_sum | solution.py:492
  3.9 61.5 %whole.1 = f32[16,2048]{1,0:T(8,128)} custom-call(s32[128]{0:T(128)} %select_reduce_fusion.refs_0_, s32[18]{0:T(128)} %dynamic-slice_reduce_fusion.refs_1_, s32[1]{0:T(128)S(6)} %copy.12.refs_2_, s32[1]{0:T(128)S(6)} %copy.13.refs_3_, f32[18,16,128]{2,1,0:T(8,128)} %refs_4_.1, f32[16,2048]{1,0:T(8,128)} %refs_5_.1, ...), custom_call_target="tpu_custom_call" | custom-call | tf_op jit(solution)/shard_map/whole/pallas_call | solution.py:450
  65.4 1.6 %copy.14 = f32[16,2048]{1,0:T(8,128)} copy(f32[16,2048]{1,0:T(8,128)} %whole.1) | data formatting | bytes 262144

commit v4 on v3

--- a/solution.py
+++ b/solution.py
@@ -84,10 +84,19 @@
 def column_powers():
     u = 2.0 * (np.arange(COLS).astype(np.float32) + np.float32(0.5)) / np.float32(COLS) - np.float32(1.0)
     u = u.astype(np.float32)
-    return np.stack([u, u * u] + [np.zeros_like(u)] * 6)
-
-
-def fit_stage(shift, first_row, own, above, below, sci, band, va, vb, upow, e_out, mom_out, rolled, hs, acc):
+    return u
+
+
+def column_rows():
+    return np.stack([column_powers()] * 8)
+
+
+def column_factors():
+    u = column_powers()
+    return to_bf16(np.concatenate([np.stack([u ** (k + 1)] * 16) for k in range(4)]))
+
+
+def fit_stage(shift, first_row, own, above, below, sci, band, va, vb, powers, e_out, mom_out, rolled, hs, acc, last):
     start = CM + shift - H
     tile = lax.shift_right_logical(start, 7)
     rem = lax.bitwise_and(start, 127)
@@ -127,44 +136,50 @@
                 hs[f * SLOTS : (f + 1) * SLOTS, j * TC : (j + 1) * TC] = res[
                     j * SLOTS : (j + 1) * SLOTS, o : o + TC
                 ]
+    sub8 = lax.broadcasted_iota(jnp.int32, (8, 1), 0)
     for c in range(8):
         cols = slice(256 * c, 256 * c + 256)
         oa = jnp.dot(va[...], hs[0:208, cols].astype(BF16), preferred_element_type=F32)
         ob = jnp.dot(vb[...], hs[200:440, cols].astype(BF16), preferred_element_type=F32)
-        e = jnp.concatenate([oa.reshape(ROWS, 16, 256), ob.reshape(ROWS, 16, 256)], axis=1)
-        e_out[:, cols] = e.reshape(ROWS * 32, 256).astype(BF16)
+        pieces = []
+        for r in range(ROWS):
+            pieces += [
+                oa[16 * r : 16 * r + 16],
+                ob[16 * r : 16 * r + 8],
+                jnp.where(sub8 == TARGET - 24, sci[r : r + 1, cols], ob[16 * r + 8 : 16 * r + 16]),
+            ]
+        e_out[:, cols] = jnp.concatenate(pieces, axis=0).astype(BF16)
     acc[...] = jnp.zeros_like(acc)
-    u1 = upow[0:1, :]
-    u2 = upow[1:2, :]
-    brow = lax.broadcasted_iota(jnp.int32, (32, 1), 0)
 
     def row_step(r, carry):
-        e = e_out[pl.ds(pl.multiple_of(r * 32, 32), 32), :].astype(F32)
-        e = jnp.where(brow == TARGET, sci[pl.ds(r, 1), :], e)
-        e16 = e.astype(BF16)
-        e = e16.astype(F32)
-        f1 = (e * u1).astype(BF16)
-        f2 = (e * u2).astype(BF16)
+        e = e_out[pl.ds(pl.multiple_of(r * 32, 32), 32), :]
+        rows = [e]
+        for k in range(4):
+            p = powers[16 * k : 16 * k + 16, :]
+            rows += [e[0:16] * p, e[16:32] * p]
         g = lax.dot_general(
-            jnp.concatenate([e16, f2], axis=0),
-            jnp.concatenate([e16, f1, f2], axis=0),
+            e,
+            jnp.concatenate(rows, axis=0),
             (((1,), (1,)), ((), ())),
             preferred_element_type=F32,
         )
         v = (first_row + r).astype(F32) * (2.0 / 256.0) + (1.0 / 256.0 - 1.0)
-        scale = 1.0
-        for m in range(5):
-            n = 64 if m < 2 else 32
-            acc[m, 0:n, 0:96] += g[0:n] * scale
+        last[:, 0:32] += g[:, TC : TC + 32]
+        g = g[:, 0:TC]
+        scale = v
+        acc[0] += g
+        for m in range(1, 5):
+            acc[m] += g * scale
             scale = scale * v
         return carry
 
-    lax.fori_loop(0, ROWS, row_step, 0)
+    last[...] = jnp.zeros_like(last)
+    lax.fori_loop(0, ROWS, row_step, 0, unroll=4)
     units = (
-        jnp.where(lane < 96, acc[0, 0:32], pltpu.roll(acc[0, 32:64], 64, 1)),
-        jnp.where(lane < 96, acc[1, 0:32], pltpu.roll(acc[1, 32:64], 64, 1)),
-        jnp.where(lane < 96, acc[2, 0:32], pltpu.roll(acc[0, 32:64], 32, 1)),
-        jnp.where(lane < 64, acc[3, 0:32], pltpu.roll(acc[4, 0:32], 64, 1)),
+        acc[0],
+        acc[1],
+        jnp.where(lane < 96, acc[2], pltpu.roll(last[...], 96, 1)),
+        jnp.where(lane < 64, acc[3], pltpu.roll(acc[4], 64, 1)),
     )
     for i, unit in enumerate(units):
         for j in range(4):
@@ -209,7 +224,7 @@
     ]
 
 
-def sweep_panel(mat, fx, q, lane):
+def sweep_panel(mat, zero, q, lane):
     t = q // 4
     top = 32 * q
     base = 32 * (q % 4)
@@ -221,7 +236,11 @@
             [jnp.broadcast_to(tiles[i][t][:, l0 + j : l0 + j + 1], (8, TC)) for j in range(4)]
             for i in range(4)
         ]
-        p = [[jnp.broadcast_to(cols[i0][j][s0 + i : s0 + i + 1], (8, TC)) for j in range(4)] for i in range(4)]
+        whole_cols = [cols[i0][j] + zero for j in range(4)]
+        p = [
+            [jnp.broadcast_to(whole_cols[j][s0 + i : s0 + i + 1], (8, TC)) for j in range(4)]
+            for i in range(4)
+        ]
         w = inverse4(p)
         in_lane = (lane >= l0) & (lane < l0 + 4)
         in_row = (sub >= s0) & (sub < s0 + 4)
@@ -245,8 +264,8 @@
                     old = jnp.where(in_row, 0.0, old)
                 u = rows[h]
                 tiles[i][h] = old - ((c[0] * u[0] + c[1] * u[1]) + (c[2] * u[2] + c[3] * u[3]))
-    fx[...] = jnp.zeros_like(fx)
     inside = (lane >= base) & (lane < base + 28)
+    swept = [[], []]
     for i in range(4):
         for h in range(2):
             f = tiles[i][h]
@@ -254,9 +273,33 @@
                 f = jnp.where(inside, -f, f)
             if i == 3:
                 f = jnp.where(sub < 4, f, 0.0)
-            fx[base + 8 * i : base + 8 * i + 8, TC * h : TC * h + TC] = f
-    rest = mat[top + 32 : 200, TC * t : TC * t + TC]
-    change = jnp.dot(rest, fx[...], preferred_element_type=F32, precision=lax.Precision.HIGHEST)
+            swept[h].append(f)
+    f = jnp.concatenate([jnp.concatenate(swept[h], axis=0) for h in range(2)], axis=1)
+    f_hi = f.astype(BF16)
+    f = f - f_hi.astype(F32)
+    f_mid = f.astype(BF16)
+    f_lo = (f - f_mid.astype(F32)).astype(BF16)
+    right = jnp.concatenate(
+        [f_hi, f_mid, f_hi, f_lo, f_hi, f_mid, jnp.zeros((64, 2 * TC), BF16)], axis=0
+    )
+    z = jnp.where(inside, mat[top + 32 : 200, TC * t : TC * t + TC], 0.0)
+    if base:
+        z = pltpu.roll(z, 128 - base, 1)
+    z = z + pltpu.roll(z, 32, 1)
+    z = z + pltpu.roll(z, 64, 1)
+    z_hi = z.astype(BF16).astype(F32)
+    z = z - z_hi
+    z_mid = z.astype(BF16).astype(F32)
+    z_lo = z - z_mid
+    slot = lax.shift_right_logical(lane, 5)
+    left = jnp.concatenate(
+        [
+            jnp.where(slot == 2, z_mid, z_hi),
+            jnp.where(slot == 0, z_lo, jnp.where(slot == 1, z_mid, 0.0)),
+        ],
+        axis=1,
+    ).astype(BF16)
+    change = jnp.dot(left, right, preferred_element_type=F32)
     for h in range(2):
         old = mat[top + 32 : 200, TC * h : TC * h + TC]
         if h == t:
@@ -294,8 +337,10 @@
             mat[32 * q : 32 * q + 32, TC * t : TC * t + TC] = block
             if q == 0:
                 mat[192:200, TC * t : TC * t + TC] = jnp.where(col_active(t), block[24:32], 0.0)
+    fx[...] = jnp.zeros_like(fx)
+    zero = fx[...]
     for q in range(6):
-        sweep_panel(mat, fx, q, lane)
+        sweep_panel(mat, zero, q, lane)
     coef = []
     for q in range(6):
         z = mat[192:200, TC * (q // 4) : TC * (q // 4) + TC]
@@ -320,7 +365,7 @@
         los.append((wide_p - h.astype(F32)).astype(BF16))
     res = jnp.dot(jnp.concatenate(his + los, axis=0), e_ref[...], preferred_element_type=F32)
     t0, t1, t2 = (res[16 * i : 16 * i + 16] + res[48 + 16 * i : 64 + 16 * i] for i in range(3))
-    u = upow[0:1, :]
+    u = jnp.concatenate([upow[...]] * 2, axis=0)
     out[...] = sci[...] - (t0 + u * (t1 + u * t2))
 
 
@@ -328,8 +373,8 @@
 
 
 def whole_kernel(
-    ccds, strips, pick, owner, shift, order, store, sci_h, band_h, va_h, vb_h, upow_h, out,
-    sent, got, own, edge, sci, band, va, vb, upow, e, rolled, hs, acc, mom, parts, part, totals, mat, fx,
+    ccds, strips, pick, owner, shift, order, store, sci_h, band_h, va_h, vb_h, upow_h, powers_h, out,
+    sent, got, own, edge, sci, band, va, vb, upow, powers, e, rolled, hs, acc, last, mom, parts, part, totals, mat, fx,
     local, send, recv, esend, erecv, s1, r1, s2, r2,
 ):
     ccd = lax.axis_index("ccd")
@@ -340,18 +385,26 @@
     loads = [
         pltpu.make_async_copy(h, v, local.at[i])
         for i, (h, v) in enumerate(
-            ((band_h, band), (va_h, va), (vb_h, vb), (upow_h, upow), (sci_h, sci))
+            ((band_h, band), (va_h, va), (vb_h, vb), (upow_h, upow), (powers_h, powers), (sci_h, sci))
         )
     ]
 
-    def peer(k):
-        return lax.rem(ccd + k // strips, ccds), lax.rem(strip + lax.rem(k, strips), strips)
-
-    def greet(k, carry):
-        pl.semaphore_signal(barrier, inc=1, device_id=peer(k), device_id_type=MESH)
-        return carry
-
-    lax.fori_loop(1, count, greet, 0)
+    beside = [lax.rem(strip + k, strips) for k in range(strips)]
+
+    def each_peer(act):
+        def plane(i, carry):
+            to = lax.rem(ccd + ccds - 1 - i, ccds)
+            for k in range(strips - 1, -1, -1):
+                act(to, beside[k])
+            return carry
+
+        lax.fori_loop(0, ccds - 1, plane, 0)
+        for k in range(strips - 1, 0, -1):
+            act(ccd, beside[k])
+
+    each_peer(
+        lambda c, k: pl.semaphore_signal(barrier, inc=1, device_id=(c, k), device_id_type=MESH)
+    )
     for load in loads:
         load.start()
 
@@ -363,19 +416,16 @@
     got[me] = sent[me]
     pl.semaphore_wait(barrier, count - 1)
 
-    def push(k, carry):
-        to = peer(k)
-        pltpu.make_async_remote_copy(
-            src_ref=sent.at[to[0] * strips + to[1]],
+    each_peer(
+        lambda c, k: pltpu.make_async_remote_copy(
+            src_ref=sent.at[c * strips + k],
             dst_ref=got.at[me],
             send_sem=send,
             recv_sem=recv,
-            device_id=to,
+            device_id=(c, k),
             device_id_type=MESH,
         ).start()
-        return carry
-
-    lax.fori_loop(1, count, push, 0)
+    )
     rest = got.at[pl.ds(0, count - 1)]
     pltpu.make_async_copy(rest, rest, recv).wait()
     for t in range(own.shape[0]):
@@ -400,8 +450,8 @@
     above = jnp.where(strip > 0, edge[0], 0.0)
     below = jnp.where(strip < strips - 1, edge[1], 0.0)
     first_row = strip * ROWS
-    fit_stage(shift[0], first_row, own, above, below, sci, band, va, vb, upow, e, mom, rolled, hs, acc)
-    peers = [(ccd, lax.rem(strip + k, strips)) for k in range(1, strips)]
+    fit_stage(shift[0], first_row, own, above, below, sci, band, va, vb, powers, e, mom, rolled, hs, acc, last)
+    peers = [(ccd, k) for k in beside[1:]]
     for to in peers:
         pltpu.make_async_remote_copy(
             src_ref=mom.at[to[1]],
@@ -444,13 +494,13 @@
 def whole(pick, owner, shift, order, store, sci, ccds, strips):
     count = ccds * strips
     tiles = (owner.shape[0], *store.shape[1:])
-    tables = [band_matrix(), *vertical_matrices(), column_powers()]
+    tables = [band_matrix(), *vertical_matrices(), column_rows(), column_factors()]
     blocks = pltpu.VMEM((strips, 128 // strips, TC), F32)
     dma = pltpu.SemaphoreType.DMA
     return pl.pallas_call(
         lambda *refs: whole_kernel(ccds, strips, *refs),
         out_shape=jax.ShapeDtypeStruct((ROWS, COLS), F32),
-        in_specs=[SM] * 4 + [VM] + [ANY] * 5,
+        in_specs=[SM] * 4 + [VM] + [ANY] * 6,
         out_specs=VM,
         scratch_shapes=[
             pltpu.VMEM((count, *store.shape[1:]), F32),
@@ -462,14 +512,15 @@
             pltpu.VMEM((ROWS * 32, COLS), BF16),
             pltpu.VMEM((tiles[0] + 1, SLOTS, TC), F32),
             pltpu.VMEM((440, COLS), F32),
-            pltpu.VMEM((5, 64, TC), F32),
+            pltpu.VMEM((5, 32, TC), F32),
+            pltpu.VMEM((32, TC), F32),
             blocks,
             blocks,
             pltpu.VMEM((128 // strips, TC), F32),
             blocks,
             pltpu.VMEM((200, 2 * TC), F32),
-            pltpu.VMEM((TC, 2 * TC), F32),
-            dma((5,)),
+            pltpu.VMEM((8, TC), F32),
+            dma((6,)),
             dma,
             dma,
             dma((2,)),

time: 67.3 us -> 62 us (0.921)
  Pallas kernels: 61.5 us -> 56.2 us
    pallas_call x1, Pallas kernels: 61.5 us -> 56.2 us  [whole(): pl.pallas_call(lambda *refs: whole_kernel(ccds, strips, *refs), out_shape...]
where the time goes in v4:
time: 62 us; the launch traced here: 61.7 us
  Pallas kernels  56.2 us (91%)
  local copies, waits for them, and re-layouts  2.97 us (5%)
  between operations  1.31 us (2%)
  other arithmetic  1.25 us (2%)
    pallas_call x1, Pallas kernels, whole(): pl.pallas_call(lambda *refs: whole_kernel(ccds, strips, *refs), out_shape...  56.2 us
    unnamed x1, local copies, waits for them, and re-layouts  1.57 us
    dynamic_slice x1, local copies, waits for them, and re-layouts, body(): owner = lax.dynamic_index_in_dim(tile_source, me, 0, keepdims=False)  1.4 us
    reduce_sum x1, other arithmetic, body(): pick = jnp.sum(jnp.where(tile_source == me, tile_slot, 0), axis=1)  1.25 us

profile of v4, /device:TPU:0, one launch (start us, length us, event | category | flops | bytes accessed | tf_op | source)
XLA Modules:
  0.0 61.7 jit_solution(17987931167661369234)
XLA Ops:
  1.3 1.4 %dynamic-slice_reduce_fusion.refs_1_ = s32[18]{0:T(128)} fusion(s32[128,18]{0,1:T(8,128)} %param.12, s32[]{:T(128)S(6)} %select_n.9), kind=kLoop, calls=%fused_computation | loop fusion | bytes 148 | tf_op jit(solution)/shard_map/jit(dynamic_index_in_dim)/dynamic_slice | solution.py:544
  2.7 1.2 %select_reduce_fusion.refs_0_ = s32[128]{0:T(128)} fusion(s32[128,18]{0,1:T(8,128)} %param.13, s32[128,18]{0,1:T(8,128)} %param.12, s32[]{:T(128)S(6)} %add.7), kind=kLoop, calls=%fused_computation.1 | loop fusion | flops 6784 | bytes 18948 | tf_op jit(solution)/shard_map/reduce_sum | solution.py:543
  3.9 56.2 %whole.1 = f32[16,2048]{1,0:T(8,128)} custom-call(s32[128]{0:T(128)} %select_reduce_fusion.refs_0_, s32[18]{0:T(128)} %dynamic-slice_reduce_fusion.refs_1_, s32[1]{0:T(128)S(6)} %copy.13.refs_2_, s32[1]{0:T(128)S(6)} %copy.14.refs_3_, f32[18,16,128]{2,1,0:T(8,128)} %refs_4_.1, f32[16,2048]{1,0:T(8,128)} %refs_5_.1, ...), custom_call_target="tpu_custom_call" | custom-call | tf_op jit(solution)/shard_map/whole/pallas_call | solution.py:500
  60.1 1.6 %copy.15 = f32[16,2048]{1,0:T(8,128)} copy(f32[16,2048]{1,0:T(8,128)} %whole.1) | data formatting | bytes 262144

commit v5 on v4

--- a/solution.py
+++ b/solution.py
@@ -373,9 +373,9 @@
 
 
 def whole_kernel(
-    ccds, strips, pick, owner, shift, order, store, sci_h, band_h, va_h, vb_h, upow_h, powers_h, out,
+    ccds, strips, shift, order, source, slot, store, sci_h, band_h, va_h, vb_h, upow_h, powers_h, out,
     sent, got, own, edge, sci, band, va, vb, upow, powers, e, rolled, hs, acc, last, mom, parts, part, totals, mat, fx,
-    local, send, recv, esend, erecv, s1, r1, s2, r2,
+    table, index, local, index_sem, send, recv, esend, erecv, s1, r1, s2, r2,
 ):
     ccd = lax.axis_index("ccd")
     strip = lax.axis_index("strip")
@@ -390,17 +390,16 @@
     ]
 
     beside = [lax.rem(strip + k, strips) for k in range(strips)]
+    hops = (0, 1, 2, 1)
+    turn = lambda i, k: lax.rem(i + k, 4)
+    shifts = [(y, c, z, x) for y in range(4) for c in range(2) for z in range(4) for x in range(4)]
+    shifts.sort(key=lambda o: -(hops[o[0]] + hops[o[2]] + hops[o[3]] + 0.5 * o[1]))
+    rows = [[turn(ccd // 2, y) * 2 + lax.rem(ccd + c, 2) for c in range(2)] for y in range(4)]
+    cells = [[turn(strip // 4, z) * 4 + turn(lax.rem(strip, 4), x) for x in range(4)] for z in range(4)]
 
     def each_peer(act):
-        def plane(i, carry):
-            to = lax.rem(ccd + ccds - 1 - i, ccds)
-            for k in range(strips - 1, -1, -1):
-                act(to, beside[k])
-            return carry
-
-        lax.fori_loop(0, ccds - 1, plane, 0)
-        for k in range(strips - 1, 0, -1):
-            act(ccd, beside[k])
+        for y, c, z, x in shifts[:-1]:
+            act(rows[y][c], cells[z][x])
 
     each_peer(
         lambda c, k: pl.semaphore_signal(barrier, inc=1, device_id=(c, k), device_id_type=MESH)
@@ -408,8 +407,17 @@
     for load in loads:
         load.start()
 
+    tiles = source.shape[0]
+    pick = jnp.sum(jnp.where(source[...] == me, slot[...], 0), axis=0, keepdims=True)
+    table[0:8] = jnp.broadcast_to(pick, (8, count))
+    table[24:32] = jnp.zeros((8, count), jnp.int32)
+    table[8 : 8 + tiles] = source[...]
+    to_index = pltpu.make_async_copy(table, index, index_sem)
+    to_index.start()
+    to_index.wait()
+
     def choose(d, carry):
-        sent[d] = store[pick[d]]
+        sent[d] = store[index[0, d]]
         return carry
 
     lax.fori_loop(0, count, choose, 0, unroll=8)
@@ -429,7 +437,7 @@
     rest = got.at[pl.ds(0, count - 1)]
     pltpu.make_async_copy(rest, rest, recv).wait()
     for t in range(own.shape[0]):
-        own[t] = got[owner[t]]
+        own[t] = got[index[8 + t, me]]
     edges = [
         pltpu.make_async_remote_copy(
             src_ref=own,
@@ -491,16 +499,16 @@
 LIMIT = 60 * 1024 * 1024
 
 
-def whole(pick, owner, shift, order, store, sci, ccds, strips):
+def whole(shift, order, source, slot, store, sci, ccds, strips):
     count = ccds * strips
-    tiles = (owner.shape[0], *store.shape[1:])
+    tiles = (source.shape[0], *store.shape[1:])
     tables = [band_matrix(), *vertical_matrices(), column_rows(), column_factors()]
     blocks = pltpu.VMEM((strips, 128 // strips, TC), F32)
     dma = pltpu.SemaphoreType.DMA
     return pl.pallas_call(
         lambda *refs: whole_kernel(ccds, strips, *refs),
-        out_shape=jax.ShapeDtypeStruct((ROWS, COLS), F32),
-        in_specs=[SM] * 4 + [VM] + [ANY] * 6,
+        out_shape=pltpu.VMEM((ROWS, COLS), F32),
+        in_specs=[SM] * 2 + [VM] * 3 + [ANY] * 6,
         out_specs=VM,
         scratch_shapes=[
             pltpu.VMEM((count, *store.shape[1:]), F32),
@@ -520,7 +528,10 @@
             blocks,
             pltpu.VMEM((200, 2 * TC), F32),
             pltpu.VMEM((8, TC), F32),
+            pltpu.VMEM((32, count), jnp.int32),
+            pltpu.SMEM((32, count), jnp.int32),
             dma((6,)),
+            dma,
             dma,
             dma,
             dma((2,)),
@@ -534,16 +545,14 @@
             collective_id=0, has_side_effects=True, vmem_limit_bytes=LIMIT
         ),
         name="whole",
-    )(pick, owner, shift, order, store, sci, *[jnp.asarray(x) for x in tables])
+    )(shift, order, source, slot, store, sci, *[jnp.asarray(x) for x in tables])
 
 
 def body(tile_store, tile_source, tile_slot, shift_cols, spatial_order, science):
     strips = lax.axis_size("strip")
-    me = lax.axis_index("ccd") * strips + lax.axis_index("strip")
-    pick = jnp.sum(jnp.where(tile_source == me, tile_slot, 0), axis=1)
-    owner = lax.dynamic_index_in_dim(tile_source, me, 0, keepdims=False)
     return whole(
-        pick, owner, shift_cols, spatial_order, tile_store, science, lax.axis_size("ccd"), strips
+        shift_cols, spatial_order, tile_source.T, tile_slot.T, tile_store, science,
+        lax.axis_size("ccd"), strips,
     )
 
 

time: 62 us -> 55.3 us (0.89)
  Pallas kernels: 56.2 us -> 53.2 us
  local copies, waits for them, and re-layouts: 2.97 us -> 0.66 us
  other arithmetic: 1.25 us -> 0 us
    pallas_call x1, Pallas kernels: 56.2 us -> 53.2 us  [whole(): pl.pallas_call(lambda *refs: whole_kernel(ccds, strips, *refs), out_shape...]
    dynamic_slice x1 -> x0, local copies, waits for them, and re-layouts: 1.4 us -> none  [body(): owner = lax.dynamic_index_in_dim(tile_source, me, 0, keepdims=False)]
    reduce_sum x1 -> x0, other arithmetic: 1.25 us -> none  [body(): pick = jnp.sum(jnp.where(tile_source == me, tile_slot, 0), axis=1)]
    unnamed x1, local copies, waits for them, and re-layouts: 1.57 us -> 0.66 us
where the time goes in v5:
time: 55.3 us; the launch traced here: 55.2 us
  Pallas kernels  53.2 us (96%)
  between operations  1.3 us (2%)
  local copies, waits for them, and re-layouts  0.66 us (1%)
    pallas_call x1, Pallas kernels, whole(): pl.pallas_call(lambda *refs: whole_kernel(ccds, strips, *refs), out_shape...  53.2 us

profile of v5, /device:TPU:0, one launch (start us, length us, event | category | flops | bytes accessed | tf_op | source)
XLA Modules:
  0.0 55.2 jit_solution(2982512677871130006)
XLA Ops:
  1.3 53.2 %whole.1 = f32[16,2048]{1,0:T(8,128)S(1)} custom-call(s32[1]{0:T(128)S(6)} %copy.14.refs_0_, s32[1]{0:T(128)S(6)} %copy.15.refs_1_, s32[18,128]{1,0:T(8,128)} %bitcast.2, s32[18,128]{1,0:T(8,128)} %bitcast.3, f32[18,16,128]{2,1,0:T(8,128)} %refs_4_.1, f32[16,2048]{1,0:T(8,128)} %refs_5_.1, bf16[512,1408]{1,0:T(8,128)(2,1)} %constant.10.clone.refs_6_, ...), custom_call_target="tpu_custom_call" | custom-call | tf_op jit(solution)/shard_map/whole/pallas_call | solution.py:508
  54.5 0.7 %copy.13 = f32[16,2048]{1,0:T(8,128)} copy(f32[16,2048]{1,0:T(8,128)S(1)} %whole.1) | data formatting | bytes 262144

commit v6 on v5

--- a/solution.py
+++ b/solution.py
@@ -96,26 +96,35 @@
     return to_bf16(np.concatenate([np.stack([u ** (k + 1)] * 16) for k in range(4)]))
 
 
-def fit_stage(shift, first_row, own, above, below, sci, band, va, vb, powers, e_out, mom_out, rolled, hs, acc, last):
+def pack_rows(x):
+    pairs = x.reshape(x.shape[0] // 2, 2, 16, TC)
+    a, b = pairs[:, 0], pairs[:, 1]
+    row = lax.broadcasted_iota(jnp.int32, (1, 8, TC), 1)
+    mid = jnp.where(row < 3, a[:, 8:], pltpu.roll(b[:, :8], 3, 1))
+    return jnp.concatenate([a[:, :8], mid, pltpu.roll(b, H, 1)[:, :8]], axis=1)
+
+
+def unpack_rows(x):
+    row = lax.broadcasted_iota(jnp.int32, (1, 8, TC), 1)
+    end = pltpu.roll(x[:, 16:], 5, 1)
+    b = jnp.concatenate([jnp.where(row < 5, pltpu.roll(x[:, 8:16], 5, 1), end), end], axis=1)
+    pairs = jnp.concatenate([x[:, None, :16], b[:, None]], axis=1)
+    return pairs.reshape(2 * x.shape[0], 16, TC)
+
+
+def window_rows(shift, x, first, rolled, hs, band):
+    count, rows, _ = x.shape
     start = CM + shift - H
     tile = lax.shift_right_logical(start, 7)
     rem = lax.bitwise_and(start, 127)
-    count = own.shape[0]
-    row16 = lax.broadcasted_iota(jnp.int32, (1, 16, TC), 1)
-    row8 = lax.broadcasted_iota(jnp.int32, (1, 8, TC), 1)
-    a = pltpu.roll(above, H, 1)
-    b = pltpu.roll(below, H, 1)
-    mid = jnp.where(row16 < H, a, b)
-    end = jnp.where(row8 < 6, b[:, :8], jnp.where(row8 == 6, 1.0, 0.0))
-    x = jnp.concatenate([own[...], mid, end], axis=1)
-    rolled[0:count] = pltpu.roll(x, lax.bitwise_and(128 - rem, 127), 2)
-    rolled[count : count + 1] = jnp.zeros((1, SLOTS, TC), F32)
-    lane3 = lax.broadcasted_iota(jnp.int32, (1, SLOTS, TC), 2)
+    rolled[0:count, 0:rows] = pltpu.roll(x, lax.bitwise_and(128 - rem, 127), 2)
+    rolled[count : count + 1, 0:rows] = jnp.zeros((1, rows, TC), F32)
+    lane3 = lax.broadcasted_iota(jnp.int32, (1, rows, TC), 2)
     w = jnp.where(
-        lane3 < 128 - rem, rolled[pl.ds(tile, 17)], rolled[pl.ds(tile + 1, 17)]
-    ).reshape(17 * SLOTS, TC)
-    main = w[: 16 * SLOTS]
-    nxt = w[SLOTS:]
+        lane3 < 128 - rem, rolled[pl.ds(tile, 17), 0:rows], rolled[pl.ds(tile + 1, 17), 0:rows]
+    ).reshape(17 * rows, TC)
+    main = w[: 16 * rows]
+    nxt = w[rows:]
     hi = main.astype(BF16)
     lo = (main - hi.astype(F32)).astype(BF16)
     nhi = nxt.astype(BF16).astype(F32)
@@ -133,9 +142,19 @@
         for f in range(2 * c, 2 * c + n // TC):
             o = (f - 2 * c) * TC
             for j in range(16):
-                hs[f * SLOTS : (f + 1) * SLOTS, j * TC : (j + 1) * TC] = res[
-                    j * SLOTS : (j + 1) * SLOTS, o : o + TC
+                hs[f * SLOTS + first : f * SLOTS + first + rows, j * TC : (j + 1) * TC] = res[
+                    j * rows : (j + 1) * rows, o : o + TC
                 ]
+
+
+def fit_stage(shift, first_row, above, below, sci, band, va, vb, powers, e_out, mom_out, rolled, hs, acc, last):
+    row16 = lax.broadcasted_iota(jnp.int32, (1, 16, TC), 1)
+    row8 = lax.broadcasted_iota(jnp.int32, (1, 8, TC), 1)
+    lane = lax.broadcasted_iota(jnp.int32, (1, TC), 1)
+    b = pltpu.roll(below, H, 1)
+    mid = jnp.where(row16 < H, above, b)
+    end = jnp.where(row8 < 6, b[:, :8], jnp.where(row8 == 6, 1.0, 0.0))
+    window_rows(shift, jnp.concatenate([mid, end], axis=1), ROWS, rolled, hs, band)
     sub8 = lax.broadcasted_iota(jnp.int32, (8, 1), 0)
     for c in range(8):
         cols = slice(256 * c, 256 * c + 256)
@@ -373,9 +392,9 @@
 
 
 def whole_kernel(
-    ccds, strips, shift, order, source, slot, store, sci_h, band_h, va_h, vb_h, upow_h, powers_h, out,
+    ccds, strips, shift_h, order_h, source_h, slot_h, store_h, sci_h, band_h, va_h, vb_h, upow_h, powers_h, out,
     sent, got, own, edge, sci, band, va, vb, upow, powers, e, rolled, hs, acc, last, mom, parts, part, totals, mat, fx,
-    table, index, local, index_sem, send, recv, esend, erecv, s1, r1, s2, r2,
+    shift, order, source, slot, store, packed, table, index, local, index_sem, send, recv, esend, erecv, s1, r1, s2, r2,
 ):
     ccd = lax.axis_index("ccd")
     strip = lax.axis_index("strip")
@@ -385,11 +404,11 @@
     loads = [
         pltpu.make_async_copy(h, v, local.at[i])
         for i, (h, v) in enumerate(
-            ((band_h, band), (va_h, va), (vb_h, vb), (upow_h, upow), (powers_h, powers), (sci_h, sci))
+            ((source_h, source), (slot_h, slot), (store_h, store), (shift_h, shift), (order_h, order),
+             (band_h, band), (va_h, va), (vb_h, vb), (upow_h, upow), (powers_h, powers), (sci_h, sci))
         )
     ]
 
-    beside = [lax.rem(strip + k, strips) for k in range(strips)]
     hops = (0, 1, 2, 1)
     turn = lambda i, k: lax.rem(i + k, 4)
     shifts = [(y, c, z, x) for y in range(4) for c in range(2) for z in range(4) for x in range(4)]
@@ -406,6 +425,8 @@
     )
     for load in loads:
         load.start()
+    for load in loads[:3]:
+        load.wait()
 
     tiles = source.shape[0]
     pick = jnp.sum(jnp.where(source[...] == me, slot[...], 0), axis=0, keepdims=True)
@@ -438,9 +459,11 @@
     pltpu.make_async_copy(rest, rest, recv).wait()
     for t in range(own.shape[0]):
         own[t] = got[index[8 + t, me]]
+    packed[0] = pack_rows(pltpu.roll(own[...], 16 - 5, 1))
+    packed[1] = pack_rows(own[...])
     edges = [
         pltpu.make_async_remote_copy(
-            src_ref=own,
+            src_ref=packed.at[way],
             dst_ref=edge.at[way],
             send_sem=esend.at[way],
             recv_sem=erecv.at[way],
@@ -451,15 +474,16 @@
     ]
     for copy in edges:
         copy.start()
-    for load in loads:
+    for load in loads[3:]:
         load.wait()
+    window_rows(shift[0], own[...], 0, rolled, hs, band)
     for copy in edges:
         copy.wait()
-    above = jnp.where(strip > 0, edge[0], 0.0)
-    below = jnp.where(strip < strips - 1, edge[1], 0.0)
+    above = jnp.where(strip > 0, unpack_rows(edge[0]), 0.0)
+    below = jnp.where(strip < strips - 1, unpack_rows(edge[1]), 0.0)
     first_row = strip * ROWS
-    fit_stage(shift[0], first_row, own, above, below, sci, band, va, vb, powers, e, mom, rolled, hs, acc, last)
-    peers = [(ccd, k) for k in beside[1:]]
+    fit_stage(shift[0], first_row, above, below, sci, band, va, vb, powers, e, mom, rolled, hs, acc, last)
+    peers = [(ccd, cells[z][x]) for y, c, z, x in shifts[:-1] if y == 0 and c == 0]
     for to in peers:
         pltpu.make_async_remote_copy(
             src_ref=mom.at[to[1]],
@@ -508,17 +532,17 @@
     return pl.pallas_call(
         lambda *refs: whole_kernel(ccds, strips, *refs),
         out_shape=pltpu.VMEM((ROWS, COLS), F32),
-        in_specs=[SM] * 2 + [VM] * 3 + [ANY] * 6,
+        in_specs=[ANY] * 11,
         out_specs=VM,
         scratch_shapes=[
             pltpu.VMEM((count, *store.shape[1:]), F32),
             pltpu.VMEM((count, *store.shape[1:]), F32),
             pltpu.VMEM(tiles, F32),
-            pltpu.VMEM((2, *tiles), F32),
+            pltpu.VMEM((2, tiles[0] // 2, 24, TC), F32),
             pltpu.VMEM((ROWS, COLS), F32),
             *[pltpu.VMEM(x.shape, x.dtype) for x in tables],
             pltpu.VMEM((ROWS * 32, COLS), BF16),
-            pltpu.VMEM((tiles[0] + 1, SLOTS, TC), F32),
+            pltpu.VMEM((tiles[0] + 1, SLOTS - ROWS, TC), F32),
             pltpu.VMEM((440, COLS), F32),
             pltpu.VMEM((5, 32, TC), F32),
             pltpu.VMEM((32, TC), F32),
@@ -528,9 +552,15 @@
             blocks,
             pltpu.VMEM((200, 2 * TC), F32),
             pltpu.VMEM((8, TC), F32),
+            pltpu.SMEM((1,), jnp.int32),
+            pltpu.SMEM((1,), jnp.int32),
+            pltpu.VMEM(source.shape, jnp.int32),
+            pltpu.VMEM(source.shape, jnp.int32),
+            pltpu.VMEM(store.shape, F32),
+            pltpu.VMEM((2, tiles[0] // 2, 24, TC), F32),
             pltpu.VMEM((32, count), jnp.int32),
             pltpu.SMEM((32, count), jnp.int32),
-            dma((6,)),
+            dma((11,)),
             dma,
             dma,
             dma,

time: 55.3 us -> 52.9 us (0.957)
  Pallas kernels: 53.2 us -> 50.8 us
    pallas_call x1, Pallas kernels: 53.2 us -> 50.8 us  [whole(): pl.pallas_call(lambda *refs: whole_kernel(ccds, strips, *refs), out_shape...]
where the time goes in v6:
time: 52.9 us; the launch traced here: 52.8 us
  Pallas kernels  50.8 us (96%)
  between operations  1.3 us (2%)
  local copies, waits for them, and re-layouts  0.66 us (1%)
    pallas_call x1, Pallas kernels, whole(): pl.pallas_call(lambda *refs: whole_kernel(ccds, strips, *refs), out_shape...  50.8 us

profile of v6, /device:TPU:0, one launch (start us, length us, event | category | flops | bytes accessed | tf_op | source)
XLA Modules:
  0.0 52.8 jit_solution(15454740677630044962)
XLA Ops:
  1.3 50.8 %whole.1 = f32[16,2048]{1,0:T(8,128)S(1)} custom-call(s32[1]{0:T(128)S(6)} %copy.14.refs_0_, s32[1]{0:T(128)S(6)} %copy.15.refs_1_, s32[18,128]{1,0:T(8,128)} %bitcast.2, s32[18,128]{1,0:T(8,128)} %bitcast.3, f32[18,16,128]{2,1,0:T(8,128)} %refs_4_.1, f32[16,2048]{1,0:T(8,128)} %refs_5_.1, bf16[512,1408]{1,0:T(8,128)(2,1)} %constant.10.clone.refs_6_, ...), custom_call_target="tpu_custom_call" | custom-call | tf_op jit(solution)/shard_map/whole/pallas_call | solution.py:532
  52.1 0.7 %copy.13 = f32[16,2048]{1,0:T(8,128)} copy(f32[16,2048]{1,0:T(8,128)S(1)} %whole.1) | data formatting | bytes 262144

commit v7 on v6

--- a/solution.py
+++ b/solution.py
@@ -112,7 +112,7 @@
     return pairs.reshape(2 * x.shape[0], 16, TC)
 
 
-def window_rows(shift, x, first, rolled, hs, band):
+def window_rows(shift, x, rolled, hs, band):
     count, rows, _ = x.shape
     start = CM + shift - H
     tile = lax.shift_right_logical(start, 7)
@@ -142,19 +142,19 @@
         for f in range(2 * c, 2 * c + n // TC):
             o = (f - 2 * c) * TC
             for j in range(16):
-                hs[f * SLOTS + first : f * SLOTS + first + rows, j * TC : (j + 1) * TC] = res[
+                hs[f * SLOTS : f * SLOTS + rows, j * TC : (j + 1) * TC] = res[
                     j * rows : (j + 1) * rows, o : o + TC
                 ]
 
 
-def fit_stage(shift, first_row, above, below, sci, band, va, vb, powers, e_out, mom_out, rolled, hs, acc, last):
+def fit_stage(shift, first_row, own, above, below, sci, band, va, vb, powers, e_out, mom_out, rolled, hs, acc, last):
     row16 = lax.broadcasted_iota(jnp.int32, (1, 16, TC), 1)
     row8 = lax.broadcasted_iota(jnp.int32, (1, 8, TC), 1)
     lane = lax.broadcasted_iota(jnp.int32, (1, TC), 1)
     b = pltpu.roll(below, H, 1)
     mid = jnp.where(row16 < H, above, b)
     end = jnp.where(row8 < 6, b[:, :8], jnp.where(row8 == 6, 1.0, 0.0))
-    window_rows(shift, jnp.concatenate([mid, end], axis=1), ROWS, rolled, hs, band)
+    window_rows(shift, jnp.concatenate([own, mid, end], axis=1), rolled, hs, band)
     sub8 = lax.broadcasted_iota(jnp.int32, (8, 1), 0)
     for c in range(8):
         cols = slice(256 * c, 256 * c + 256)
@@ -393,8 +393,8 @@
 
 def whole_kernel(
     ccds, strips, shift_h, order_h, source_h, slot_h, store_h, sci_h, band_h, va_h, vb_h, upow_h, powers_h, out,
-    sent, got, own, edge, sci, band, va, vb, upow, powers, e, rolled, hs, acc, last, mom, parts, part, totals, mat, fx,
-    shift, order, source, slot, store, packed, table, index, local, index_sem, send, recv, esend, erecv, s1, r1, s2, r2,
+    sent, got, sent2, got2, sci, band, va, vb, upow, powers, e, rolled, hs, acc, last, mom, parts, part, totals, mat, fx,
+    shift, order, source, slot, store, local, send, recv, send2, recv2, s1, r1, s2, r2,
 ):
     ccd = lax.axis_index("ccd")
     strip = lax.axis_index("strip")
@@ -429,60 +429,81 @@
         load.wait()
 
     tiles = source.shape[0]
-    pick = jnp.sum(jnp.where(source[...] == me, slot[...], 0), axis=0, keepdims=True)
-    table[0:8] = jnp.broadcast_to(pick, (8, count))
-    table[24:32] = jnp.zeros((8, count), jnp.int32)
-    table[8 : 8 + tiles] = source[...]
-    to_index = pltpu.make_async_copy(table, index, index_sem)
-    to_index.start()
-    to_index.wait()
-
-    def choose(d, carry):
-        sent[d] = store[index[0, d]]
-        return carry
-
-    lax.fori_loop(0, count, choose, 0, unroll=8)
-    got[me] = sent[me]
+    flat = tiles * ROWS
+    sheet = jnp.concatenate([store[...].reshape(flat, TC), jnp.zeros((-flat % TC, TC), F32)], axis=0)
+    near = sheet.shape[0] // TC
+    for i in range(near):
+        sent[pl.ds(i, count, stride=near), :] = jnp.transpose(sheet[TC * i : TC * i + TC])
+    for i in range(near):
+        got[pl.ds(near * me + i, 1), :] = sent[pl.ds(near * me + i, 1), :]
     pl.semaphore_wait(barrier, count - 1)
 
-    each_peer(
-        lambda c, k: pltpu.make_async_remote_copy(
-            src_ref=sent.at[c * strips + k],
-            dst_ref=got.at[me],
-            send_sem=send,
-            recv_sem=recv,
-            device_id=(c, k),
-            device_id_type=MESH,
-        ).start()
-    )
-    rest = got.at[pl.ds(0, count - 1)]
+    def send_all(src, dst, size, done, arrived):
+        each_peer(
+            lambda c, k: pltpu.make_async_remote_copy(
+                src_ref=src.at[pl.ds(size * (c * strips + k), size)],
+                dst_ref=dst.at[pl.ds(size * me, size)],
+                send_sem=done,
+                recv_sem=arrived,
+                device_id=(c, k),
+                device_id_type=MESH,
+            ).start()
+        )
+
+    send_all(sent, got, near, send, recv)
+    rest = got.at[pl.ds(0, near * (count - 1))]
     pltpu.make_async_copy(rest, rest, recv).wait()
-    for t in range(own.shape[0]):
-        own[t] = got[index[8 + t, me]]
-    packed[0] = pack_rows(pltpu.roll(own[...], 16 - 5, 1))
-    packed[1] = pack_rows(own[...])
-    edges = [
-        pltpu.make_async_remote_copy(
-            src_ref=packed.at[way],
-            dst_ref=edge.at[way],
-            send_sem=esend.at[way],
-            recv_sem=erecv.at[way],
-            device_id=(ccd, lax.rem(strip + (1 if way == 0 else strips - 1), strips)),
-            device_id_type=MESH,
-        )
-        for way in range(2)
-    ]
-    for copy in edges:
-        copy.start()
+    sheet = jnp.concatenate(
+        [jnp.transpose(got[pl.ds(i, count, stride=near), :]) for i in range(near)], axis=0
+    )
+    found = []
+    for t in range(tiles):
+        owner = jnp.broadcast_to(source[t : t + 1, :], (8, count))
+        place = jnp.broadcast_to(slot[t : t + 1, :], (8, count))
+        for h in range(0, ROWS, 8):
+            tile = jnp.zeros((8, count), F32)
+            for p in range(tiles):
+                tile = jnp.where(
+                    place == p,
+                    jnp.take_along_axis(
+                        sheet[ROWS * p + h : ROWS * p + h + 8], owner, axis=1, mode="promise_in_bounds"
+                    ),
+                    tile,
+                )
+            found.append(tile)
+    mine = jnp.concatenate(found, axis=0)
+    up = pack_rows(pltpu.roll(pltpu.roll(mine, 1, 1).reshape(tiles, ROWS, count), 16 - 5, 1))
+    down = pack_rows(pltpu.roll(mine, count - 1, 1).reshape(tiles, ROWS, count))
+    half = tiles // 2 * 24
+    sheet = jnp.concatenate(
+        [
+            mine,
+            up.reshape(half, count),
+            down.reshape(half, count),
+            jnp.zeros((-(flat + 2 * half) % TC, count), F32),
+        ],
+        axis=0,
+    )
+    far = sheet.shape[0] // TC
+    for i in range(far):
+        sent2[pl.ds(i, count, stride=far), :] = jnp.transpose(sheet[TC * i : TC * i + TC])
+    send_all(sent2, got2, far, send2, recv2)
+    for i in range(far):
+        got2[pl.ds(far * me + i, 1), :] = sent2[pl.ds(far * me + i, 1), :]
     for load in loads[3:]:
         load.wait()
-    window_rows(shift[0], own[...], 0, rolled, hs, band)
-    for copy in edges:
-        copy.wait()
-    above = jnp.where(strip > 0, unpack_rows(edge[0]), 0.0)
-    below = jnp.where(strip < strips - 1, unpack_rows(edge[1]), 0.0)
+    rest2 = got2.at[pl.ds(0, far * (count - 1))]
+    pltpu.make_async_copy(rest2, rest2, recv2).wait()
+    sheet = jnp.concatenate(
+        [jnp.transpose(got2[pl.ds(i, count, stride=far), :]) for i in range(far)], axis=0
+    )
+    own = sheet[:flat].reshape(tiles, ROWS, TC)
+    above = unpack_rows(sheet[flat : flat + half].reshape(tiles // 2, 24, TC))
+    below = unpack_rows(sheet[flat + half : flat + 2 * half].reshape(tiles // 2, 24, TC))
+    above = jnp.where(strip > 0, above, 0.0)
+    below = jnp.where(strip < strips - 1, below, 0.0)
     first_row = strip * ROWS
-    fit_stage(shift[0], first_row, above, below, sci, band, va, vb, powers, e, mom, rolled, hs, acc, last)
+    fit_stage(shift[0], first_row, own, above, below, sci, band, va, vb, powers, e, mom, rolled, hs, acc, last)
     peers = [(ccd, cells[z][x]) for y, c, z, x in shifts[:-1] if y == 0 and c == 0]
     for to in peers:
         pltpu.make_async_remote_copy(
@@ -513,6 +534,7 @@
     pltpu.make_async_copy(few, few, r2).wait()
     apply_stage(order[0], first_row, totals, e, sci, upow, out, mat, fx)
     pltpu.make_async_copy(rest, rest, send).wait()
+    pltpu.make_async_copy(rest2, rest2, send2).wait()
     pltpu.make_async_copy(few, few, s1).wait()
     pltpu.make_async_copy(few, few, s2).wait()
 
@@ -525,7 +547,9 @@
 
 def whole(shift, order, source, slot, store, sci, ccds, strips):
     count = ccds * strips
-    tiles = (source.shape[0], *store.shape[1:])
+    tiles = source.shape[0]
+    near = -(-tiles * ROWS // TC)
+    far = -(-(tiles * ROWS + tiles * 24) // TC)
     tables = [band_matrix(), *vertical_matrices(), column_rows(), column_factors()]
     blocks = pltpu.VMEM((strips, 128 // strips, TC), F32)
     dma = pltpu.SemaphoreType.DMA
@@ -535,14 +559,14 @@
         in_specs=[ANY] * 11,
         out_specs=VM,
         scratch_shapes=[
-            pltpu.VMEM((count, *store.shape[1:]), F32),
-            pltpu.VMEM((count, *store.shape[1:]), F32),
-            pltpu.VMEM(tiles, F32),
-            pltpu.VMEM((2, tiles[0] // 2, 24, TC), F32),
+            pltpu.VMEM((near * count, TC), F32),
+            pltpu.VMEM((near * count, TC), F32),
+            pltpu.VMEM((far * count, TC), F32),
+            pltpu.VMEM((far * count, TC), F32),
             pltpu.VMEM((ROWS, COLS), F32),
             *[pltpu.VMEM(x.shape, x.dtype) for x in tables],
             pltpu.VMEM((ROWS * 32, COLS), BF16),
-            pltpu.VMEM((tiles[0] + 1, SLOTS - ROWS, TC), F32),
+            pltpu.VMEM((tiles + 1, SLOTS, TC), F32),
             pltpu.VMEM((440, COLS), F32),
             pltpu.VMEM((5, 32, TC), F32),
             pltpu.VMEM((32, TC), F32),
@@ -557,15 +581,11 @@
             pltpu.VMEM(source.shape, jnp.int32),
             pltpu.VMEM(source.shape, jnp.int32),
             pltpu.VMEM(store.shape, F32),
-            pltpu.VMEM((2, tiles[0] // 2, 24, TC), F32),
-            pltpu.VMEM((32, count), jnp.int32),
-            pltpu.SMEM((32, count), jnp.int32),
             dma((11,)),
             dma,
             dma,
             dma,
-            dma((2,)),
-            dma((2,)),
+            dma,
             dma,
             dma,
             dma,

time: 52.9 us -> 49.5 us (0.936)
  Pallas kernels: 50.8 us -> 47.4 us
    pallas_call x1, Pallas kernels: 50.8 us -> 47.4 us  [whole(): pl.pallas_call(lambda *refs: whole_kernel(ccds, strips, *refs), out_shape...]
where the time goes in v7:
time: 49.5 us; the launch traced here: 49.4 us
  Pallas kernels  47.4 us (96%)
  between operations  1.3 us (3%)
  local copies, waits for them, and re-layouts  0.66 us (1%)
    pallas_call x1, Pallas kernels, whole(): pl.pallas_call(lambda *refs: whole_kernel(ccds, strips, *refs), out_shape...  47.4 us

profile of v7, /device:TPU:0, one launch (start us, length us, event | category | flops | bytes accessed | tf_op | source)
XLA Modules:
  0.0 49.4 jit_solution(7835568977757899123)
XLA Ops:
  1.3 47.4 %whole.1 = f32[16,2048]{1,0:T(8,128)S(1)} custom-call(s32[1]{0:T(128)S(6)} %copy.14.refs_0_, s32[1]{0:T(128)S(6)} %copy.15.refs_1_, s32[18,128]{1,0:T(8,128)} %bitcast.2, s32[18,128]{1,0:T(8,128)} %bitcast.3, f32[18,16,128]{2,1,0:T(8,128)} %refs_4_.1, f32[16,2048]{1,0:T(8,128)} %refs_5_.1, bf16[512,1408]{1,0:T(8,128)(2,1)} %constant.10.clone.refs_6_, ...), custom_call_target="tpu_custom_call" | custom-call | tf_op jit(solution)/shard_map/whole/pallas_call | solution.py:556
  48.8 0.7 %copy.13 = f32[16,2048]{1,0:T(8,128)} copy(f32[16,2048]{1,0:T(8,128)S(1)} %whole.1) | data formatting | bytes 262144
